TPU v7x, 32 devices: a whole 2x2x4 slice. The times are simulated.
32 devices in a mesh: dp: 8 (over z, y), tensor: 4 (over x, core).
Axes of the slice: x: 2, y: 2, z: 4, core: 2. Of those that a mesh axis runs over, the one named last changes fastest.
Arguments:
- hidden: bfloat16 [4096, 4096], P('dp'), may hold values from -40 to 40
- q_weight: bfloat16 [8192, 1024], P('dp', 'tensor'), may hold values from -0.09375 to 0.09375
- kv_weight: bfloat16 [8192, 512], P('dp', 'tensor'), may hold values from -0.09375 to 0.09375
- owner: int32 [4], replicated, may hold values from 0 to 1
- lengths: int32 [16], P('dp'), may hold values from 64 to 256, as said below
Outputs:
- attended: bfloat16 [4096, 1024], P('dp', 'tensor')
Inputs may be any that keep to these rules, and one draw needn't show every extreme that they name: `lengths`: some sequence has length exactly 256.
All inputs are finite; a program needn't handle non-finite values.
Results may differ from a plain program's by a relative error of at most 0.0092.
Values may be sent and summed in bfloat16 or wider, within the bound.
No kernel may reach another device: no remote copies, remote signals or barrier semaphores. Data moves between devices by JAX's collectives and lax.ppermute only.
A program may use at most 64 MiB of HBM per device.

v0:
```python
import math

import jax
import jax.numpy as jnp
from jax import lax
from jax.sharding import PartitionSpec as P

HEAD_DIM = 128
SEQ_LEN = 256
OLD_DATA = 4


def spread(value, axis, root):
    mine = lax.axis_index(axis) == root
    return lax.psum(jnp.where(mine, value, jnp.zeros_like(value)), axis)


def from_partner(value, axis, stride):
    mask = 2**stride
    pairs = [(source, source ^ mask) for source in range(lax.axis_size(axis))]
    return lax.ppermute(value, axis, pairs)


def rotate(values, positions, columns, active):
    pair_index = columns % HEAD_DIM // 2
    inverse = jnp.exp(-(2.0 * pair_index.astype(jnp.float32) / HEAD_DIM) * math.log(10000.0))
    angles = positions.astype(jnp.float32)[:, None] * inverse[None, :]
    signs = jnp.where(columns % 2 == 0, -1.0, 1.0).astype(jnp.float32)
    swapped = values.reshape(values.shape[0], -1, 2)[:, :, ::-1].reshape(values.shape)
    turned = values * jnp.cos(angles) + swapped * (jnp.sin(angles) * signs[None, :])
    return jnp.where(active[None, :], turned, values)


def body(hidden, q_weight, kv_weight, owner, lengths):
    row_count = hidden.shape[0]
    q_blocks = []
    kv_blocks = []
    for quarter in range(OLD_DATA):
        root_rank = owner[quarter] * OLD_DATA + quarter
        fetched_q, fetched_kv = (
            spread(q_weight, "dp", root_rank),
            spread(kv_weight, "dp", root_rank),
        )
        q_blocks.append(fetched_q)
        kv_blocks.append(fetched_kv)
    queries = jnp.dot(hidden, jnp.concatenate(q_blocks, axis=0), preferred_element_type=jnp.float32)
    keyvals = jnp.dot(
        hidden, jnp.concatenate(kv_blocks, axis=0), preferred_element_type=jnp.float32
    )
    positions = jnp.arange(row_count) % SEQ_LEN
    tensor_index = lax.axis_index("tensor")
    kv_width = kv_weight.shape[1]
    q_columns = jnp.arange(queries.shape[1])
    queries = rotate(queries, positions, q_columns, q_columns >= 0).astype(jnp.bfloat16)
    kv_columns = tensor_index * kv_width + jnp.arange(kv_width)
    keyvals = rotate(keyvals, positions, kv_columns, kv_columns // HEAD_DIM % 2 == 0).astype(
        jnp.bfloat16
    )
    partner = from_partner(keyvals, "tensor", 0)
    is_even = tensor_index % 2 == 0
    key_rows = jnp.where(is_even, keyvals, partner)
    value_rows = jnp.where(is_even, partner, keyvals)
    seq_count = row_count // SEQ_LEN
    per_device = queries.shape[1] // HEAD_DIM
    key_block = key_rows.reshape(seq_count, SEQ_LEN, HEAD_DIM)
    value_block = value_rows.reshape(seq_count, SEQ_LEN, HEAD_DIM)
    query_block = queries.reshape(seq_count, SEQ_LEN, per_device, HEAD_DIM)
    key_spots = jnp.arange(SEQ_LEN)
    allowed = (key_spots[None, None, :] <= key_spots[None, :, None]) & (
        key_spots[None, None, :] < lengths[:, None, None]
    )
    scores = jnp.einsum(
        "sqhd,skd->shqk", query_block, key_block, preferred_element_type=jnp.float32
    ) / math.sqrt(HEAD_DIM)
    scores = jnp.where(allowed[:, None, :, :], scores, -1e30)
    row_max = jnp.max(scores, axis=-1, keepdims=True)
    raised = jnp.exp(scores - row_max)
    row_total = jnp.sum(raised, axis=-1, keepdims=True)
    probs = (raised / row_total).astype(jnp.bfloat16)
    mixed = jnp.einsum("shqk,skd->sqhd", probs, value_block, preferred_element_type=jnp.float32)
    return mixed.astype(jnp.bfloat16).reshape(row_count, per_device * HEAD_DIM)


def solution(mesh):
    return jax.shard_map(
        body,
        mesh=mesh,
        in_specs=(P("dp", None), P("dp", "tensor"), P("dp", "tensor"), P(), P("dp")),
        out_specs=P("dp", "tensor"),
        check_vma=False,
    )
```

profile of v0, /device:TPU:0, one launch (start us, length us, event | category | flops | bytes accessed | tf_op | source)
XLA Modules:
  0.0 170.9 jit_solution(3968873753242986457)
XLA Ops:
  6.5 0.0 all-reduce.3.cloned.1.call-start
  6.5 1.5 fusion.51
  10.5 2.4 %broadcast_select_fusion.3 = (bf16[1024,256]{1,0:T(8,128)(2,1)}, bf16[1024,256]{1,0:T(8,128)(2,1)}, bf16[1024,256]{1,0:T(8,128)(2,1)}, bf16[1024,256]{1,0:T(8,128)(2,1)}) fusion(bf16[1024,256]{1,0:T(8,128)(2,1)} %param.6, pred[]{:T(512)S(6)} %eq.53, pred[]{:T(512)S(6)} %eq.54, pred[]{:T(512)S(6)} %eq.56, pred[]{:T(512)S(6)} %eq.55), kind=kLoop, calls=%fused_computation.36 | loop fusion | flops 1048576 | bytes 2621444 | tf_op jit(solution)/shard_map/jit(_where)/select_n | solution.py:15
  12.9 1.9 %broadcast_select_fusion.7 = (bf16[1024,128]{1,0:T(8,128)(2,1)}, bf16[1024,128]{1,0:T(8,128)(2,1)}, bf16[1024,128]{1,0:T(8,128)(2,1)}, bf16[1024,128]{1,0:T(8,128)(2,1)}) fusion(bf16[1024,128]{1,0:T(8,128)(2,1)} %param.7, pred[]{:T(512)S(6)} %eq.53, pred[]{:T(512)S(6)} %eq.54, pred[]{:T(512)S(6)} %eq.56, pred[]{:T(512)S(6)} %eq.55), kind=kLoop, calls=%fused_computation.52 | loop fusion | flops 524288 | bytes 1310724 | tf_op jit(solution)/shard_map/jit(_where)/select_n | solution.py:15
  14.8 0.0 all-reduce.3.cloned.1.call-update
  15.0 0.0 copy-done.4
  15.0 0.1 iota_compare_fusion.1
  15.1 0.1 broadcast_and_fusion
  15.2 131.7 %all-reduce.3.cloned.1.call-done = (bf16[1024,128]{1,0:T(8,128)(2,1)}, bf16[1024,128]{1,0:T(8,128)(2,1)}, bf16[1024,128]{1,0:T(8,128)(2,1)}, bf16[1024,128]{1,0:...) async-done(((bf16[1024,128]{1,0:T(8,128)(2,1)}, bf16[1024,128]{1,0:T(8,128)(2,1)}, ...) | async-done | bytes 3145744 | tf_op jit(solution)/shard_map/psum | solution.py:15
  146.9 4.2 %fusion.13 = f32[512,256]{0,1:T(8,128)S(1)} fusion(bf16[512,4096]{1,0:T(8,128)(2,1)} %param.5, bf16[1024,256]{1,0:T(8,128)(2,1)} %get-tuple-element.9, bf16[1024,256]{1,0:T(8,128)(2,1)} %get-tuple-element.10, bf16[1024,256]{1,0:T(8,128)(2,1)} %get-tuple-element.11, bf16[1024,256]{1,0:T(8,128)(2,1)} %get-tuple-element.12), kind=kOutput, calls=%fused_computation.14 | convolution fusion | flops 1082130432 | bytes 6815744 | tf_op jit(solution)/shard_map/dot_general | solution.py:46
  151.1 0.3 reshape.210
  151.4 1.4 rev.7
  152.8 0.4 reshape.211
  153.2 0.0 copy-done
  153.2 0.0 copy-done.1
  153.2 0.0 copy-done.2
  153.2 0.0 copy-done.3
  153.3 3.7 %convolution_bitcast_fusion = f32[512,128]{0,1:T(8,128)S(1)} fusion(bf16[512,4096]{1,0:T(8,128)(2,1)} %param.5, bf16[1024,128]{1,0:T(8,128)(2,1)S(1)} %copy-done, bf16[1024,128]{1,0:T(8,128)(2,1)S(1)} %copy-done.1, bf16[1024,128]{1,0:T(8,128)(2,1)S(1)} %copy-done.2, bf16[1024,128]{1,0:T(8,128)(2,1)S(1)} %copy-done.3), kind=kOutput, calls=%fused_computation.17 | convolution fusion | flops 541065216 | bytes 5505024 | tf_op jit(solution)/shard_map/dot_general | solution.py:47
  157.0 0.1 reshape.206
  157.1 0.7 rev.6
  157.9 0.2 reshape.207
  158.1 1.2 fusion.32
  159.3 0.1 collective-permute-start
  159.4 2.3 %fusion.26 = bf16[512,256]{0,1:T(8,128)(2,1)S(1)} fusion(f32[512,256]{0,1:T(8,128)S(1)} %fusion.13, f32[512,256]{0,1:T(8,128)S(1)} %reshape.211, f32[256]{0:T(256)S(1)} %get-tuple-element.29, f32[256]{0:T(256)S(1)} %get-tuple-element.30, f32[512]{0:T(512)S(1)} %fusion.39), kind=kLoop, calls=%fused_computation.30 | loop fusion | flops 786432 | bytes 1314816 | tf_op jit(solution)/shard_map/convert_element_type | solution.py:54
  161.7 0.1 reshape.212
  161.7 0.0 collective-permute-done
  161.8 0.1 copy.20
  161.9 0.3 fusion.12
  162.2 0.5 fusion.52
  162.7 0.4 fusion.16
  163.2 0.2 copy.14
  163.3 0.7 copy.31
  (12 shorter events, 0.2 us)
Async XLA Ops:
  6.5 8.4 %copy-start.4 = (s32[2]{0:T(128)S(1)}, s32[2]{0:T(128)}, u32[]{:S(2)}) copy-start(s32[2]{0:T(128)} %param.9) | copy-start | bytes 28
  6.5 140.4 %all-reduce.3.cloned.1.call-start = ((), (), s32[]{:S(2)}) async-start(), calls=%async_computation | async-start | bytes 6291456 | tf_op jit(solution)/shard_map/psum | solution.py:15
  146.9 6.3 %copy-start = (bf16[1024,128]{1,0:T(8,128)(2,1)S(1)}, bf16[1024,128]{1,0:T(8,128)(2,1)}, u32[]{:S(2)}) copy-start(bf16[1024,128]{1,0:T(8,128)(2,1)} %get-tuple-element.5) | copy-start | bytes 786436
  146.9 6.3 %copy-start.1 = (bf16[1024,128]{1,0:T(8,128)(2,1)S(1)}, bf16[1024,128]{1,0:T(8,128)(2,1)}, u32[]{:S(2)}) copy-start(bf16[1024,128]{1,0:T(8,128)(2,1)} %get-tuple-element.6) | copy-start | bytes 786436
  146.9 6.3 %copy-start.2 = (bf16[1024,128]{1,0:T(8,128)(2,1)S(1)}, bf16[1024,128]{1,0:T(8,128)(2,1)}, u32[]{:S(2)}) copy-start(bf16[1024,128]{1,0:T(8,128)(2,1)} %get-tuple-element.7) | copy-start | bytes 786436
  146.9 6.3 %copy-start.3 = (bf16[1024,128]{1,0:T(8,128)(2,1)S(1)}, bf16[1024,128]{1,0:T(8,128)(2,1)}, u32[]{:S(2)}) copy-start(bf16[1024,128]{1,0:T(8,128)(2,1)} %get-tuple-element.8) | copy-start | bytes 786436
  159.3 2.5 %collective-permute-start = (bf16[512,128]{0,1:T(8,128)(2,1)S(1)}, bf16[512,128]{0,1:T(8,128)(2,1)S(1)}, u32[]{:S(2)}, u32[]{:S(2)}) collective-permute-start(bf16[512,128]{0,1:T(8,128)(2,1)S(1)} %fusion.32), channel_id=1, source_target_pairs={{0,1},{1,0},{2,3},{3,2},{4,5},{5,4},{6,7},{7,6},{8,9},{9,8},{10,11... | collective-permute-start | bytes 393224 | tf_op jit(solution)/shard_map/ppermute | solution.py:21
Sparse Core Ops, SparseCore 0:
  15.0 131.8 all-reduce.2
where the time goes:
time: 171 us
  waiting for transfers between devices  132 us (77%)
  between operations  16.1 us (9%)
  matrix products  9.1 us (5%)
  other arithmetic  8.17 us (5%)
  local copies, waits for them, and re-layouts  5.75 us (3%)
    psum x1, waiting for transfers between devices, spread(): return lax.psum(jnp.where(mine, value, jnp.zeros_like(value)), axis)  132 us
    select_n x2, other arithmetic, spread(): return lax.psum(jnp.where(mine, value, jnp.zeros_like(value)), axis)  4.34 us
    dot_general x1, matrix products, body(): jnp.dot(hidden, jnp.concatenate(q_blocks, axis=0), preferred_element_type...  4.2 us
    dot_general x1, matrix products, body(): jnp.dot(hidden, jnp.concatenate(kv_blocks, axis=0), preferred_element_typ...  3.72 us
  transfers between devices with their start and end apart: 2, of which 1 were waited for; matrix products, arithmetic and copies ran while one was open for 2% of the time, Pallas kernels for 0%

commit v1 on v0

v1 whole, which is shorter than its diff:
```python
import functools
import math

import jax
import jax.numpy as jnp
from jax import lax
from jax.experimental import pallas as pl
from jax.experimental.pallas import tpu as pltpu
from jax.sharding import PartitionSpec as P


HEAD_DIM = 128
SEQ_LEN = 256
OLD_DATA = 4
IN_FLIGHT = 2


VMEM = pl.BlockSpec(memory_space=pltpu.VMEM)
SMEM = pl.BlockSpec(memory_space=pltpu.SMEM)


def swapped(value, axis, mask):
    pairs = [(source, source ^ mask) for source in range(lax.axis_size(axis))]
    return lax.ppermute(value, axis, pairs)


def near(value):
    return pltpu.with_memory_space_constraint(value, pltpu.VMEM)


def dot(left, right):
    return jnp.dot(left, right, preferred_element_type=jnp.float32)


def call(kernel, scalars, operands, outs, cost, out_specs=VMEM, spare=(), **more):
    return pl.pallas_call(
        kernel,
        out_shape=outs,
        in_specs=[SMEM] * len(scalars)
        + [VMEM] * len(operands)
        + [pl.BlockSpec(memory_space=pltpu.HBM)] * len(spare),
        out_specs=jax.tree.map(lambda _: out_specs, outs),
        compiler_params=pltpu.CompilerParams(vmem_limit_bytes=8 * 2**20),
        cost_estimate=pl.CostEstimate(flops=cost, bytes_accessed=cost // 256, transcendentals=0),
        **more,
    )(*scalars, *operands, *spare)


def tables(turned):
    columns = jnp.arange(HEAD_DIM)
    positions = jnp.arange(SEQ_LEN)
    pair_index = columns // 2
    inverse = jnp.exp(-(2.0 * pair_index.astype(jnp.float32) / HEAD_DIM) * math.log(10000.0))
    angles = positions.astype(jnp.float32)[:, None] * inverse[None, :]
    signs = jnp.where(columns % 2 == 0, -1.0, 1.0).astype(jnp.float32)
    cosine = jnp.cos(angles)
    sine = jnp.sin(angles) * signs[None, :]
    return cosine, sine, jnp.where(turned, cosine, 1.0), jnp.where(turned, sine, 0.0)


def turn(values, cosine, sine):
    lanes = lax.broadcasted_iota(jnp.int32, values.shape, 1)
    swapped = jnp.where(
        lanes % 2 == 0,
        pltpu.roll(values, values.shape[1] - 1, axis=1),
        pltpu.roll(values, 1, axis=1),
    )
    return values * cosine + swapped * sine


def attend_head(queries, keys, values, length):
    half = SEQ_LEN // 2
    scale = math.log2(math.e) / math.sqrt(HEAD_DIM)
    parts = []
    for start, stop in ((0, half), (half, SEQ_LEN)):
        rows = start + lax.broadcasted_iota(jnp.int32, (stop - start, stop), 0)
        spots = lax.broadcasted_iota(jnp.int32, (stop - start, stop), 1)
        scores = lax.dot_general(
            queries[start:stop], keys[:stop], (((1,), (1,)), ((), ())), preferred_element_type=jnp.float32
        )
        scores = jnp.where((spots <= rows) & (spots < length), scores, -1e30)
        top = jnp.max(scores, axis=-1, keepdims=True)
        raised = jnp.exp2((scores - top) * scale)
        total = jnp.sum(raised, axis=-1, keepdims=True)
        parts.append(dot(raised.astype(jnp.bfloat16), values[:stop]) / total)
    return jnp.concatenate(parts, axis=0)


def choose_kernel(keep_ref, raw_ref, other_ref, out_ref):
    @pl.when(keep_ref[0] == 1)
    def _():
        out_ref[...] = raw_ref[...]

    @pl.when(keep_ref[0] != 1)
    def _():
        out_ref[...] = other_ref[...]


def choose(keep, raw, other):
    return call(choose_kernel, [keep], [near(raw), near(other)], pltpu.VMEM(raw.shape, raw.dtype), raw.size)


def own_kernel(own_ref, mine_ref, far_ref, out_ref):
    depth = mine_ref.shape[0]
    out_ref[...] = dot(own_ref[:, :depth], mine_ref[...]) + dot(own_ref[:, depth:], far_ref[...])


def their_kernel(core_ref, first_ref, second_ref, mine_ref, far_ref, out_ref):
    half, depth = first_ref.shape[0], mine_ref.shape[0]
    mine, far = mine_ref[...], far_ref[...]
    for which, ref in ((core_ref[0], first_ref), (1 - core_ref[0], second_ref)):
        total = dot(ref[:, :depth], mine) + dot(ref[:, depth:], far)
        out_ref[pl.ds(pl.multiple_of(which * half, half), half), :] = total.astype(out_ref.dtype)


def finish_kernel(own_ref, sent_ref, cos_ref, sin_ref, out_ref):
    for seq in range(own_ref.shape[0] // SEQ_LEN):
        cut = slice(seq * SEQ_LEN, (seq + 1) * SEQ_LEN)
        total = own_ref[cut, :] + sent_ref[cut, :].astype(jnp.float32)
        out_ref[cut, :] = turn(total, cos_ref[...], sin_ref[...]).astype(out_ref.dtype)


def head_kernel(head, lengths_ref, even_ref, own_ref, sent_ref, cos_ref, sin_ref, kv_ref, partner_ref, *refs):
    is_even = even_ref[0] == 1
    out_ref, held, sems = refs[-3:]
    columns = slice(head * HEAD_DIM, (head + 1) * HEAD_DIM)
    copies = []
    for seq in range(own_ref.shape[0] // SEQ_LEN):
        cut = slice(seq * SEQ_LEN, (seq + 1) * SEQ_LEN)
        total = own_ref[cut, :] + sent_ref[cut, :].astype(jnp.float32)
        queries = turn(total, cos_ref[...], sin_ref[...]).astype(jnp.bfloat16)
        mine, partner = kv_ref[cut, :], partner_ref[cut, :]
        keys = jnp.where(is_even, mine, partner)
        values = jnp.where(is_even, partner, mine)
        held[cut, :] = attend_head(queries, keys, values, lengths_ref[seq]).astype(held.dtype)
        copies.append(pltpu.make_async_copy(held.at[cut, :], out_ref.at[cut, columns], sems.at[seq]))
        copies[-1].start()
    for copy in copies:
        copy.wait()


def two_sections(hidden, q_weight, kv_weight, owner, lengths):
    rank, tensor_index = lax.axis_index("dp"), lax.axis_index("tensor")
    quarter, core = rank % OLD_DATA, tensor_index % 2
    keep = owner[quarter] == rank // OLD_DATA
    depth, tokens = q_weight.shape[0], hidden.shape[0]
    heads = q_weight.shape[1] // HEAD_DIM
    after = lax.optimization_barrier

    half = tokens // 2
    given = lambda w: lax.dynamic_slice(hidden, (core * half, w * depth), (half, depth))
    sent = jnp.concatenate([given(quarter ^ 1), given(quarter ^ 3)], axis=1)
    whole = lambda w: lax.dynamic_slice(hidden, (0, w * depth), (tokens, depth))
    own_part = jnp.concatenate([whole(quarter), whole(quarter ^ 2)], axis=1)
    first = swapped(sent, "dp", 1)

    columns = [q_weight[:, head * HEAD_DIM : (head + 1) * HEAD_DIM] for head in range(heads)]
    blocks = [kv_weight, *after(tuple(columns))]
    others = []
    for index, raw in enumerate(blocks):
        if index >= IN_FLIGHT:
            raw, others[index - IN_FLIGHT] = after((raw, others[index - IN_FLIGHT]))
        blocks[index] = raw
        others.append(swapped(raw, "dp", OLD_DATA))
    even = (core == 0).astype(jnp.int32).reshape(1)
    core = core.astype(jnp.int32).reshape(1)
    keep = keep.astype(jnp.int32).reshape(1)
    first, turns = after((first, tables(even[0] == 1)))
    cosine, sine, key_cosine, key_sine = turns
    second = swapped(first, "tensor", 1)
    settled = []
    for raw, other in zip(blocks, others):
        mine = choose(keep, raw, other)
        settled.append((mine, swapped(mine, "dp", 2)))

    own_kv = partner = result = None
    work = 4 * tokens * depth * HEAD_DIM
    for index, (mine, far) in enumerate(settled):
        theirs = call(
            their_kernel,
            [core],
            [near(value) for value in (first, second, mine, far)],
            pltpu.VMEM((tokens, HEAD_DIM), jnp.bfloat16),
            work,
        )
        back = swapped(theirs, "dp", 1)
        own = call(
            own_kernel,
            [],
            [near(value) for value in (own_part, mine, far)],
            pltpu.VMEM((tokens, HEAD_DIM), jnp.float32),
            work,
        )
        if index == 0:
            own_kv = call(
                finish_kernel,
                [],
                [near(value) for value in (own, back, key_cosine, key_sine)],
                pltpu.VMEM((tokens, HEAD_DIM), jnp.bfloat16),
                tokens * HEAD_DIM * 8,
            )
            partner = swapped(own_kv, "tensor", 1)
            continue
        head = index - 1
        result = call(
            functools.partial(head_kernel, head),
            [lengths, even],
            [near(value) for value in (own, back, cosine, sine, own_kv, partner)],
            jax.ShapeDtypeStruct((tokens, heads * HEAD_DIM), jnp.bfloat16),
            tokens * SEQ_LEN * HEAD_DIM * 4,
            out_specs=pl.BlockSpec(memory_space=pltpu.HBM),
            scratch_shapes=[
                pltpu.VMEM((tokens, HEAD_DIM), jnp.bfloat16),
                pltpu.SemaphoreType.DMA((tokens // SEQ_LEN,)),
            ],
            spare=[] if result is None else [result],
            input_output_aliases={} if result is None else {8: 0},
        )
    return result


def many_sections(hidden, q_weight, kv_weight, owner, lengths):
    rank, tensor_index = lax.axis_index("dp"), lax.axis_index("tensor")
    sections = lax.axis_size("dp") // OLD_DATA
    quarter, core = rank % OLD_DATA, tensor_index % 2
    keep = owner[quarter] == rank // OLD_DATA
    raw = jnp.concatenate([q_weight, kv_weight], axis=1)
    same = [[s * OLD_DATA + q for s in range(sections)] for q in range(OLD_DATA)]
    mine = lax.psum(jnp.where(keep, raw, jnp.zeros_like(raw)), "dp", axis_index_groups=same)
    group = [[s * OLD_DATA + q for q in range(OLD_DATA)] for s in range(sections)]
    weight = lax.all_gather(mine, "dp", axis_index_groups=group, tiled=True)
    q_width, tokens = q_weight.shape[1], hidden.shape[0]
    seqs = tokens // SEQ_LEN
    cosine, sine, key_cosine, key_sine = tables(core == 0)

    def turned(values, cosine, sine):
        shaped = values.reshape(seqs, SEQ_LEN, -1, HEAD_DIM // 2, 2)
        swapped = shaped[..., ::-1].reshape(seqs, SEQ_LEN, -1, HEAD_DIM)
        straight = values.reshape(seqs, SEQ_LEN, -1, HEAD_DIM)
        return (straight * cosine[:, None, :] + swapped * sine[:, None, :]).astype(jnp.bfloat16)

    queries = turned(dot(hidden, weight[:, :q_width]), cosine, sine)
    own = turned(dot(hidden, weight[:, q_width:]), key_cosine, key_sine)[:, :, 0]
    partner = swapped(own, "tensor", 1)
    keys = jnp.where(core == 0, own, partner)
    values = jnp.where(core == 0, partner, own)
    spots = jnp.arange(SEQ_LEN)
    allowed = (spots[None, None, :] <= spots[None, :, None]) & (spots[None, None, :] < lengths[:, None, None])
    scores = jnp.einsum("sqhd,skd->shqk", queries, keys, preferred_element_type=jnp.float32)
    scores = jnp.where(allowed[:, None], scores / math.sqrt(HEAD_DIM), -1e30)
    raised = jnp.exp(scores - jnp.max(scores, axis=-1, keepdims=True))
    probs = (raised / jnp.sum(raised, axis=-1, keepdims=True)).astype(jnp.bfloat16)
    mixed = jnp.einsum("shqk,skd->sqhd", probs, values, preferred_element_type=jnp.float32)
    return mixed.astype(jnp.bfloat16).reshape(tokens, q_width)


def body(hidden, q_weight, kv_weight, owner, lengths):
    if lax.axis_size("dp") == 2 * OLD_DATA:
        return two_sections(hidden, q_weight, kv_weight, owner, lengths)
    return many_sections(hidden, q_weight, kv_weight, owner, lengths)


def solution(mesh):
    return jax.shard_map(
        body,
        mesh=mesh,
        in_specs=(P("dp", None), P("dp", "tensor"), P("dp", "tensor"), P(), P("dp")),
        out_specs=P("dp", "tensor"),
        check_vma=False,
    )
```

time: 171 us -> 86.4 us (0.51)
  waiting for transfers between devices: 132 us -> 50.8 us
  starting transfers between devices: 0.07 us -> 16 us
  between operations: 16.1 us -> 0.82 us
  Pallas kernels: 0 us -> 10.7 us
  matrix products: 9.1 us -> 0 us
  other arithmetic: 8.17 us -> 1.48 us
    psum x1 -> x0, waiting for transfers between devices: 132 us -> none  [spread(): return lax.psum(jnp.where(mine, value, jnp.zeros_like(value)), axis)]
    ppermute x1 -> x12, waiting for transfers between devices: 0.01 us -> 50.8 us  [swapped(): return lax.ppermute(value, axis, pairs)]
    ppermute x1 -> x12, starting transfers between devices: 0.07 us -> 16 us  [swapped(): return lax.ppermute(value, axis, pairs)]
    pallas_call x0 -> x12, Pallas kernels: none -> 10.7 us  [call(): pl.pallas_call(kernel, out_shape=outs, in_specs=[SMEM] * len(scalars) + [...]
    dot_general x4 -> x0, matrix products: 8.62 us -> none  [the longest x1 4.2 us: body(): jnp.dot(hidden, jnp.concatenate(q_blocks, axis=0), preferred_element_type...]
    dynamic_slice x0 -> x3, local copies, waits for them, and re-layouts: none -> 3.61 us  [the longest x1 1.72 us: two_sections(): whole = lambda w: lax.dynamic_slice(hidden, (0, w * depth), (tokens, depth))]
    convert_element_type x3 -> x1, other arithmetic: 3.51 us -> 0.01 us  [tables(): angles = positions.astype(jnp.float32)[:, None] * inverse[None, :]]
    select_n x5 -> x2, other arithmetic: 4.4 us -> 1.22 us  [the longest x1 1.21 us: tables(): jnp.where(turned, sine, 0.0)]
  transfers between devices with their start and end apart: 2 -> 12, of which waited for: 1 -> 7; matrix products, arithmetic and copies ran while one was open for 2% -> 6% of each run, Pallas kernels for 0% -> 10%
where the time goes in v1:
time: 86.4 us; the launch traced here: 86.2 us
  waiting for transfers between devices  50.8 us (59%)
  starting transfers between devices  16 us (19%)
  Pallas kernels  10.7 us (12%)
  local copies, waits for them, and re-layouts  6.35 us (7%)
  other arithmetic  1.48 us (2%)
    ppermute x12, waiting for transfers between devices, swapped(): return lax.ppermute(value, axis, pairs)  50.8 us
    ppermute x12, starting transfers between devices, swapped(): return lax.ppermute(value, axis, pairs)  16 us
    pallas_call x12, Pallas kernels, call(): pl.pallas_call(kernel, out_shape=outs, in_specs=[SMEM] * len(scalars) + [...  10.7 us
  transfers between devices with their start and end apart: 12, of which 7 were waited for; matrix products, arithmetic and copies ran while one was open for 6% of the time, Pallas kernels for 10%

profile of v1, /device:TPU:0, one launch (start us, length us, event | category | flops | bytes accessed | tf_op | source)
XLA Modules:
  0.0 86.2 jit_solution(11415251547623017143)
XLA Ops:
  0.0 1.3 %fusion.6 = (bf16[256,1024]{1,0:T(8,128)(2,1)S(1)}, bf16[256,1024]{1,0:T(8,128)(2,1)S(1)}) fusion(bf16[512,4096]{1,0:T(8,128)(2,1)} %param.5, s32[]{:T(128)S(6)} %select_n.89, s32[]{:T(128)S(6)} %select_n.90, s32[]{:T(128)S(6)} %select_n.91), kind=kLoop, calls=%fused_computation.21 | loop fusion | bytes 2097164 | tf_op jit(solution)/shard_map/dynamic_slice | solution.py:151
  1.4 3.1 %collective-permute-start.3 = (bf16[256,2048]{1,0:T(8,128)(2,1)S(1)}, bf16[256,2048]{1,0:T(8,128)(2,1)S(1)}, u32[]{:S(2)}, u32[]{:S(2)}) collective-permute-start(bf16[256,2048]{1,0:T(8,128)(2,1)S(1)} %pad_maximum_fusion.1), channel_id=1, source_target_pairs={{0,4},{4,0},{8,12},{12,8},{16,20},{20,16},{24,28},{28,24},{1,5},{5... | collective-permute-start | bytes 3145736 | tf_op jit(solution)/shard_map/ppermute | solution.py:24
  4.5 1.2 %broadcast_select_fusion = (f32[256,128]{1,0:T(8,128)S(1)}, f32[256,128]{1,0:T(8,128)S(1)}, f32[256,128]{1,0:T(8,128)S(1)}, f32[256,128]{1,0:T(8,128)}) fusion(pred[]{:T(512)S(6)} %eq.27, f32[128]{0:T(128)S(1)} %get-tuple-element.33, f32[128]{0:T(128)S(1)} %get-tuple-element.34, f32[256]{0:T(256)S(1)} %iota_convert_fusion), kind=kLoop, calls=%fused_computation.5 | loop fusion | flops 131072 | bytes 526337 | tf_op jit(solution)/shard_map/jit(_where)/select_n | solution.py:58
  5.7 21.9 %collective-permute-done.3.first_ref = bf16[256,2048]{1,0:T(8,128)(2,1)S(1)} collective-permute-done((bf16[256,2048]{1,0:T(8,128)(2,1)S(1)}, bf16[256,2048]{1,0:T(8,128)(2,1)S(1)}, u32[]{:S(2)}, u32[]{:S(2)}) %collective-permute-start.3) | collective-permute-done | bytes 1048608 | tf_op jit(solution)/shard_map/ppermute | solution.py:24
  27.6 2.8 %collective-permute-start = (bf16[1024,128]{1,0:T(8,128)(2,1)S(1)}, bf16[1024,128]{1,0:T(8,128)(2,1)S(1)}, u32[]{:S(2)}, u32[]{:S(2)}) collective-permute-start(bf16[1024,128]{1,0:T(8,128)(2,1)S(1)} %copy-done.1), channel_id=1, source_target_pairs={{0,16},{4,20},{8,24},{12,28},{16,0},{20,4},{24,8},{28,12},{1,17},{... | collective-permute-start | bytes 786440 | tf_op jit(solution)/shard_map/ppermute | solution.py:24
  30.5 1.1 %fusion.7 = (bf16[1024,128]{1,0:T(8,128)(2,1)S(1)}, bf16[1024,128]{1,0:T(8,128)(2,1)S(1)}) fusion(bf16[1024,256]{1,0:T(8,128)(2,1)} %param.6), kind=kLoop, calls=%fused_computation.22 | loop fusion | bytes 1048576 | tf_op jit(solution)/shard_map/slice | solution.py:157
  31.7 0.6 dynamic_slice.17
  32.9 16.0 %collective-permute-done.other_ref = bf16[1024,128]{1,0:T(8,128)(2,1)S(1)} collective-permute-done((bf16[1024,128]{1,0:T(8,128)(2,1)S(1)}, bf16[1024,128]{1,0:T(8,128)(2,1)S(1)}, u32[]{:S(2)}, u32[]{:S(2)}) %collective-permute-start) | collective-permute-done | bytes 262176 | tf_op jit(solution)/shard_map/ppermute | solution.py:24
  49.0 0.7 copy-done.2
  49.7 0.9 %copy-done.3 = bf16[1024,128]{1,0:T(8,128)(2,1)S(1)} copy-done((bf16[1024,128]{1,0:T(8,128)(2,1)S(1)}, bf16[1024,128]{1,0:T(8,128)(2,1)}, u32[]{:S(2)}) %copy-start.3) | copy-done | bytes 262168
  50.6 3.9 %collective-permute-start.6 = (bf16[1024,128]{1,0:T(8,128)(2,1)S(1)}, bf16[1024,128]{1,0:T(8,128)(2,1)S(1)}, u32[]{:S(2)}, u32[]{:S(2)}) collective-permute-start(bf16[1024,128]{1,0:T(8,128)(2,1)S(1)} %shard_map.58.mine_ref), channel_id=1, source_target_pairs={{0,8},{4,12},{8,0},{12,4},{16,24},{20,28},{24,16},{28,20},{1,9},{5... | collective-permute-start | bytes 786440 | tf_op jit(solution)/shard_map/ppermute | solution.py:24
  54.5 1.7 %constant_dynamic-slice_fusion.1 = (bf16[512,1024]{1,0:T(8,128)(2,1)S(1)}, bf16[512,1024]{1,0:T(8,128)(2,1)S(1)}) fusion(bf16[512,4096]{1,0:T(8,128)(2,1)} %param.5, s32[]{:T(128)S(6)} %select_n.85, s32[]{:T(128)S(6)} %select_n.86), kind=kLoop, calls=%fused_computation.20 | loop fusion | bytes 4194312 | tf_op jit(solution)/shard_map/dynamic_slice | solution.py:153
  56.3 4.1 %collective-permute-done.9.other_ref = bf16[1024,128]{1,0:T(8,128)(2,1)} collective-permute-done((bf16[1024,128]{1,0:T(8,128)(2,1)S(1)}, bf16[1024,128]{1,0:T(8,128)(2,1)}, u32[]{:S(2)}, u32[]{:S(2)}) %collective-permute-start.9) | collective-permute-done | bytes 262176 | tf_op jit(solution)/shard_map/ppermute | solution.py:24
  60.4 1.0 %shard_map.62.mine_ref = bf16[1024,128]{1,0:T(8,128)(2,1)S(1)} custom-call(s32[1]{0:T(128)} %bitcast.2.keep_ref, bf16[1024,128]{1,0:T(8,128)(2,1)S(1)} %get-tuple-element.22.raw_ref, bf16[1024,128]{1,0:T(8,128)(2,1)} %collective-permute-done.9.other_ref), custom_call_target="tpu_custom_call" | custom-call | flops 131072 | bytes 512 | tf_op jit(solution)/shard_map/pallas_call | solution.py:36
  61.4 0.4 collective-permute-start.10
  61.7 4.0 %collective-permute-done.1.other_ref = bf16[1024,128]{1,0:T(8,128)(2,1)} collective-permute-done((bf16[1024,128]{1,0:T(8,128)(2,1)S(1)}, bf16[1024,128]{1,0:T(8,128)(2,1)}, u32[]{:S(2)}, u32[]{:S(2)}) %collective-permute-start.1) | collective-permute-done | bytes 262176 | tf_op jit(solution)/shard_map/ppermute | solution.py:24
  65.7 1.0 %shard_map.55.mine_ref = bf16[1024,128]{1,0:T(8,128)(2,1)S(1)} custom-call(s32[1]{0:T(128)} %bitcast.2.keep_ref, bf16[1024,128]{1,0:T(8,128)(2,1)S(1)} %get-tuple-element.15.raw_ref, bf16[1024,128]{1,0:T(8,128)(2,1)} %collective-permute-done.1.other_ref), custom_call_target="tpu_custom_call" | custom-call | flops 131072 | bytes 512 | tf_op jit(solution)/shard_map/pallas_call | solution.py:36
  66.7 0.7 collective-permute-start.2
  67.3 0.3 collective-permute-done.6.far_ref
  67.7 0.7 shard_map.60
  68.4 1.6 %collective-permute-start.7 = (bf16[512,128]{1,0:T(8,128)(2,1)S(1)}, bf16[512,128]{1,0:T(8,128)(2,1)S(1)}, u32[]{:S(2)}, u32[]{:S(2)}) collective-permute-start(bf16[512,128]{1,0:T(8,128)(2,1)S(1)} %shard_map.60), channel_id=1, source_target_pairs={{0,4},{4,0},{8,12},{12,8},{16,20},{20,16},{24,28},{28,24},{1,5},{5... | collective-permute-start | bytes 393224 | tf_op jit(solution)/shard_map/ppermute | solution.py:24
  70.2 0.7 shard_map.59.own_ref
  70.9 2.4 %collective-permute-done.10.far_ref = bf16[1024,128]{1,0:T(8,128)(2,1)S(1)} collective-permute-done((bf16[1024,128]{1,0:T(8,128)(2,1)S(1)}, bf16[1024,128]{1,0:T(8,128)(2,1)S(1)}, u32[]{:S(2)}, u32[]{:S(2)}) %collective-permute-start.10) | collective-permute-done | bytes 262176 | tf_op jit(solution)/shard_map/ppermute | solution.py:24
  73.3 0.7 shard_map.64
  74.0 1.6 %collective-permute-start.11 = (bf16[512,128]{1,0:T(8,128)(2,1)S(1)}, bf16[512,128]{1,0:T(8,128)(2,1)S(1)}, u32[]{:S(2)}, u32[]{:S(2)}) collective-permute-start(bf16[512,128]{1,0:T(8,128)(2,1)S(1)} %shard_map.64), channel_id=1, source_target_pairs={{0,4},{4,0},{8,12},{12,8},{16,20},{20,16},{24,28},{28,24},{1,5},{5... | collective-permute-start | bytes 393224 | tf_op jit(solution)/shard_map/ppermute | solution.py:24
  75.9 2.0 %collective-permute-done.2.far_ref = bf16[1024,128]{1,0:T(8,128)(2,1)S(1)} collective-permute-done((bf16[1024,128]{1,0:T(8,128)(2,1)S(1)}, bf16[1024,128]{1,0:T(8,128)(2,1)S(1)}, u32[]{:S(2)}, u32[]{:S(2)}) %collective-permute-start.2) | collective-permute-done | bytes 262176 | tf_op jit(solution)/shard_map/ppermute | solution.py:24
  78.0 0.7 shard_map.57
  78.7 1.6 %collective-permute-start.5 = (bf16[512,128]{1,0:T(8,128)(2,1)S(1)}, bf16[512,128]{1,0:T(8,128)(2,1)S(1)}, u32[]{:S(2)}, u32[]{:S(2)}) collective-permute-start(bf16[512,128]{1,0:T(8,128)(2,1)S(1)} %shard_map.57), channel_id=1, source_target_pairs={{0,4},{4,0},{8,12},{12,8},{16,20},{20,16},{24,28},{28,24},{1,5},{5... | collective-permute-start | bytes 393224 | tf_op jit(solution)/shard_map/ppermute | solution.py:24
  80.3 0.7 shard_map.63.own_ref
  81.0 0.7 shard_map.56.own_ref
  81.8 2.2 %shard_map.65.refs_0_ = bf16[512,256]{1,0:T(8,128)(2,1)} custom-call(s32[2]{0:T(128)S(1)} %copy-done.4, s32[1]{0:T(128)} %bitcast.even_ref, f32[512,128]{1,0:T(8,128)S(1)} %shard_map.63.own_ref, bf16[512,128]{1,0:T(8,128)(2,1)S(1)} %collective-permute-done.11.sent_ref, f32[256,128]{1,0:T(8,128)S(1)} %get-tuple-element.17.cos_ref, ...), custom_call_target="tpu_custom_call" | custom-call | flops 67108864 | bytes 262144 | tf_op jit(solution)/shard_map/pallas_call | solution.py:36
  84.0 2.2 %shard_map.66 = bf16[512,256]{1,0:T(8,128)(2,1)} custom-call(s32[2]{0:T(128)S(1)} %copy-done.4, s32[1]{0:T(128)} %bitcast.even_ref, f32[512,128]{1,0:T(8,128)S(1)} %shard_map.56.own_ref, bf16[512,128]{1,0:T(8,128)(2,1)S(1)} %collective-permute-done.5.sent_ref, f32[256,128]{1,0:T(8,128)S(1)} %get-tuple-element.17.cos_ref, ...), custom_call_target="tpu_custom_call", output_to_operand_aliasing={{}: (8, {})} | custom-call | flops 67108864 | bytes 262144 | tf_op jit(solution)/shard_map/pallas_call | solution.py:36
  (25 shorter events, 0.8 us)
Async XLA Ops:
  0.0 27.6 %copy-start.1 = (bf16[1024,128]{1,0:T(8,128)(2,1)S(1)}, bf16[1024,128]{1,0:T(8,128)(2,1)}, u32[]{:S(2)}) copy-start(bf16[1024,128]{1,0:T(8,128)(2,1)} %raw_ref.1) | copy-start | bytes 786436
  1.3 30.4 %copy-start.5 = (s32[4]{0:T(128)S(1)}, s32[4]{0:T(128)}, u32[]{:S(2)}) copy-start(s32[4]{0:T(128)} %param.8) | copy-start | bytes 52
  1.4 26.2 %collective-permute-start.3 = (bf16[256,2048]{1,0:T(8,128)(2,1)S(1)}, bf16[256,2048]{1,0:T(8,128)(2,1)S(1)}, u32[]{:S(2)}, u32[]{:S(2)}) collective-permute-start(bf16[256,2048]{1,0:T(8,128)(2,1)S(1)} %pad_maximum_fusion.1), channel_id=1, source_target_pairs={{0,4},{4,0},{8,12},{12,8},{16,20},{20,16},{24,28},{28,24},{1,5},{5... | collective-permute-start | bytes 3145736 | tf_op jit(solution)/shard_map/ppermute | solution.py:24
  27.6 40.0 %collective-permute-start.4 = (bf16[256,2048]{1,0:T(8,128)(2,1)S(1)}, bf16[256,2048]{1,0:T(8,128)(2,1)S(1)}, u32[]{:S(2)}, u32[]{:S(2)}) collective-permute-start(bf16[256,2048]{1,0:T(8,128)(2,1)S(1)} %collective-permute-done.3.first_ref), channel_id=1, source_target_pairs={{0,1},{1,0},{2,3},{3,2},{4,5},{5,4},{6,7},{7,6},{8,9},{9,8},{10,11... | collective-permute-start | bytes 3145736 | tf_op jit(solution)/shard_map/ppermute | solution.py:24
  27.6 21.3 %collective-permute-start = (bf16[1024,128]{1,0:T(8,128)(2,1)S(1)}, bf16[1024,128]{1,0:T(8,128)(2,1)S(1)}, u32[]{:S(2)}, u32[]{:S(2)}) collective-permute-start(bf16[1024,128]{1,0:T(8,128)(2,1)S(1)} %copy-done.1), channel_id=1, source_target_pairs={{0,16},{4,20},{8,24},{12,28},{16,0},{20,4},{24,8},{28,12},{1,17},{... | collective-permute-start | bytes 786440 | tf_op jit(solution)/shard_map/ppermute | solution.py:24
  31.5 28.9 %collective-permute-start.9 = (bf16[1024,128]{1,0:T(8,128)(2,1)S(1)}, bf16[1024,128]{1,0:T(8,128)(2,1)}, u32[]{:S(2)}, u32[]{:S(2)}) collective-permute-start(bf16[1024,128]{1,0:T(8,128)(2,1)S(1)} %get-tuple-element.22.raw_ref), channel_id=1, source_target_pairs={{0,16},{4,20},{8,24},{12,28},{16,0},{20,4},{24,8},{28,12},{1,17},{... | collective-permute-start | bytes 786440 | tf_op jit(solution)/shard_map/ppermute | solution.py:24
  49.0 0.7 copy-start.2
  49.7 16.1 %collective-permute-start.1 = (bf16[1024,128]{1,0:T(8,128)(2,1)S(1)}, bf16[1024,128]{1,0:T(8,128)(2,1)}, u32[]{:S(2)}, u32[]{:S(2)}) collective-permute-start(bf16[1024,128]{1,0:T(8,128)(2,1)S(1)} %get-tuple-element.15.raw_ref), channel_id=1, source_target_pairs={{0,16},{4,20},{8,24},{12,28},{16,0},{20,4},{24,8},{28,12},{1,17},{... | collective-permute-start | bytes 786440 | tf_op jit(solution)/shard_map/ppermute | solution.py:24
  49.7 1.0 %copy-start.3 = (bf16[1024,128]{1,0:T(8,128)(2,1)S(1)}, bf16[1024,128]{1,0:T(8,128)(2,1)}, u32[]{:S(2)}) copy-start(bf16[1024,128]{1,0:T(8,128)(2,1)} %copy-done.2) | copy-start | bytes 786436
  50.6 17.0 %collective-permute-start.6 = (bf16[1024,128]{1,0:T(8,128)(2,1)S(1)}, bf16[1024,128]{1,0:T(8,128)(2,1)S(1)}, u32[]{:S(2)}, u32[]{:S(2)}) collective-permute-start(bf16[1024,128]{1,0:T(8,128)(2,1)S(1)} %shard_map.58.mine_ref), channel_id=1, source_target_pairs={{0,8},{4,12},{8,0},{12,4},{16,24},{20,28},{24,16},{28,20},{1,9},{5... | collective-permute-start | bytes 786440 | tf_op jit(solution)/shard_map/ppermute | solution.py:24
  61.4 11.9 %collective-permute-start.10 = (bf16[1024,128]{1,0:T(8,128)(2,1)S(1)}, bf16[1024,128]{1,0:T(8,128)(2,1)S(1)}, u32[]{:S(2)}, u32[]{:S(2)}) collective-permute-start(bf16[1024,128]{1,0:T(8,128)(2,1)S(1)} %shard_map.62.mine_ref), channel_id=1, source_target_pairs={{0,8},{4,12},{8,0},{12,4},{16,24},{20,28},{24,16},{28,20},{1,9},{5... | collective-permute-start | bytes 786440 | tf_op jit(solution)/shard_map/ppermute | solution.py:24
  66.7 11.3 %collective-permute-start.2 = (bf16[1024,128]{1,0:T(8,128)(2,1)S(1)}, bf16[1024,128]{1,0:T(8,128)(2,1)S(1)}, u32[]{:S(2)}, u32[]{:S(2)}) collective-permute-start(bf16[1024,128]{1,0:T(8,128)(2,1)S(1)} %shard_map.55.mine_ref), channel_id=1, source_target_pairs={{0,8},{4,12},{8,0},{12,4},{16,24},{20,28},{24,16},{28,20},{1,9},{5... | collective-permute-start | bytes 786440 | tf_op jit(solution)/shard_map/ppermute | solution.py:24
  68.4 7.3 %collective-permute-start.7 = (bf16[512,128]{1,0:T(8,128)(2,1)S(1)}, bf16[512,128]{1,0:T(8,128)(2,1)S(1)}, u32[]{:S(2)}, u32[]{:S(2)}) collective-permute-start(bf16[512,128]{1,0:T(8,128)(2,1)S(1)} %shard_map.60), channel_id=1, source_target_pairs={{0,4},{4,0},{8,12},{12,8},{16,20},{20,16},{24,28},{28,24},{1,5},{5... | collective-permute-start | bytes 393224 | tf_op jit(solution)/shard_map/ppermute | solution.py:24
  70.9 4.7 %copy-start = (f32[256,128]{1,0:T(8,128)S(1)}, f32[256,128]{1,0:T(8,128)}, u32[]{:S(2)}) copy-start(f32[256,128]{1,0:T(8,128)} %get-tuple-element.20.cos_ref) | copy-start | bytes 393220
  74.0 7.8 %collective-permute-start.11 = (bf16[512,128]{1,0:T(8,128)(2,1)S(1)}, bf16[512,128]{1,0:T(8,128)(2,1)S(1)}, u32[]{:S(2)}, u32[]{:S(2)}) collective-permute-start(bf16[512,128]{1,0:T(8,128)(2,1)S(1)} %shard_map.64), channel_id=1, source_target_pairs={{0,4},{4,0},{8,12},{12,8},{16,20},{20,16},{24,28},{28,24},{1,5},{5... | collective-permute-start | bytes 393224 | tf_op jit(solution)/shard_map/ppermute | solution.py:24
  75.9 5.9 %collective-permute-start.8 = (bf16[512,128]{1,0:T(8,128)(2,1)S(1)}, bf16[512,128]{1,0:T(8,128)(2,1)S(1)}, u32[]{:S(2)}, u32[]{:S(2)}) collective-permute-start(bf16[512,128]{1,0:T(8,128)(2,1)S(1)} %shard_map.61.kv_ref), channel_id=1, source_target_pairs={{0,1},{1,0},{2,3},{3,2},{4,5},{5,4},{6,7},{7,6},{8,9},{9,8},{10,11... | collective-permute-start | bytes 393224 | tf_op jit(solution)/shard_map/ppermute | solution.py:24
  78.7 5.3 %collective-permute-start.5 = (bf16[512,128]{1,0:T(8,128)(2,1)S(1)}, bf16[512,128]{1,0:T(8,128)(2,1)S(1)}, u32[]{:S(2)}, u32[]{:S(2)}) collective-permute-start(bf16[512,128]{1,0:T(8,128)(2,1)S(1)} %shard_map.57), channel_id=1, source_target_pairs={{0,4},{4,0},{8,12},{12,8},{16,20},{20,16},{24,28},{28,24},{1,5},{5... | collective-permute-start | bytes 393224 | tf_op jit(solution)/shard_map/ppermute | solution.py:24
  81.0 0.8 copy-start.4

commit v2 on v1

--- a/solution.py
+++ b/solution.py
@@ -17,6 +17,7 @@
 
 VMEM = pl.BlockSpec(memory_space=pltpu.VMEM)
 SMEM = pl.BlockSpec(memory_space=pltpu.SMEM)
+ANY = pl.BlockSpec(memory_space=pl.ANY)
 
 
 def swapped(value, axis, mask):
@@ -86,18 +87,26 @@
     return jnp.concatenate(parts, axis=0)
 
 
-def choose_kernel(keep_ref, raw_ref, other_ref, out_ref):
-    @pl.when(keep_ref[0] == 1)
-    def _():
-        out_ref[...] = raw_ref[...]
-
-    @pl.when(keep_ref[0] != 1)
-    def _():
-        out_ref[...] = other_ref[...]
+def choose_kernel(keep_ref, raw_ref, other_ref, out_ref, sem):
+    for kept, ref in ((1, raw_ref), (0, other_ref)):
+
+        @pl.when(keep_ref[0] == kept)
+        def _(ref=ref):
+            copy = pltpu.make_async_copy(ref, out_ref, sem)
+            copy.start()
+            copy.wait()
 
 
 def choose(keep, raw, other):
-    return call(choose_kernel, [keep], [near(raw), near(other)], pltpu.VMEM(raw.shape, raw.dtype), raw.size)
+    return pl.pallas_call(
+        choose_kernel,
+        out_shape=pltpu.VMEM(raw.shape, raw.dtype),
+        in_specs=[SMEM, ANY, ANY],
+        out_specs=VMEM,
+        scratch_shapes=[pltpu.SemaphoreType.DMA],
+        compiler_params=pltpu.CompilerParams(vmem_limit_bytes=8 * 2**20),
+        cost_estimate=pl.CostEstimate(flops=0, bytes_accessed=4 * raw.size, transcendentals=0),
+    )(keep, raw, other)
 
 
 def own_kernel(own_ref, mine_ref, far_ref, out_ref):
@@ -159,6 +168,7 @@
     others = []
     for index, raw in enumerate(blocks):
         if index >= IN_FLIGHT:
+            raw, own_part = after((raw, own_part))
             raw, others[index - IN_FLIGHT] = after((raw, others[index - IN_FLIGHT]))
         blocks[index] = raw
         others.append(swapped(raw, "dp", OLD_DATA))

time: 86.4 us -> 76.5 us (0.89)
  waiting for transfers between devices: 50.8 us -> 37.6 us
  Pallas kernels: 10.7 us -> 15.3 us
  local copies, waits for them, and re-layouts: 6.35 us -> 4.81 us
    ppermute x12, waiting for transfers between devices: 50.8 us -> 37.6 us  [swapped(): return lax.ppermute(value, axis, pairs)]
    pallas_call x0 -> x3, Pallas kernels: none -> 2.88 us  [choose(): pl.pallas_call(choose_kernel, out_shape=pltpu.VMEM(raw.shape, raw.dtype),...]
    pallas_call x12 -> x9, Pallas kernels: 10.7 us -> 12.5 us  [call(): pl.pallas_call(kernel, out_shape=outs, in_specs=[SMEM] * len(scalars) + [...]
    unnamed x12 -> x8, local copies, waits for them, and re-layouts: 1.67 us -> 0.28 us
  transfers between devices with their start and end apart: 12 -> 12, of which waited for: 7 -> 5; matrix products, arithmetic and copies ran while one was open for 6% -> 6% of each run, Pallas kernels for 10% -> 17%
where the time goes in v2:
time: 76.5 us; the launch traced here: 76.1 us
  waiting for transfers between devices  37.6 us (49%)
  starting transfers between devices  16 us (21%)
  Pallas kernels  15.3 us (20%)
  local copies, waits for them, and re-layouts  4.81 us (6%)
  other arithmetic  1.48 us (2%)
  between operations  0.88 us (1%)
    ppermute x12, waiting for transfers between devices, swapped(): return lax.ppermute(value, axis, pairs)  37.6 us
    ppermute x12, starting transfers between devices, swapped(): return lax.ppermute(value, axis, pairs)  16 us
    pallas_call x9, Pallas kernels, call(): pl.pallas_call(kernel, out_shape=outs, in_specs=[SMEM] * len(scalars) + [...  12.5 us
    pallas_call x3, Pallas kernels, choose(): pl.pallas_call(choose_kernel, out_shape=pltpu.VMEM(raw.shape, raw.dtype),...  2.88 us
    dynamic_slice x1, local copies, waits for them, and re-layouts, two_sections(): whole = lambda w: lax.dynamic_slice(hidden, (0, w * depth), (tokens, depth))  1.72 us
  transfers between devices with their start and end apart: 12, of which 5 were waited for; matrix products, arithmetic and copies ran while one was open for 6% of the time, Pallas kernels for 17%

profile of v2, /device:TPU:0, one launch (start us, length us, event | category | flops | bytes accessed | tf_op | source)
XLA Modules:
  0.0 76.1 jit_solution(6149841697918937793)
XLA Ops:
  0.0 1.3 %fusion.6 = (bf16[256,1024]{1,0:T(8,128)(2,1)S(1)}, bf16[256,1024]{1,0:T(8,128)(2,1)S(1)}) fusion(bf16[512,4096]{1,0:T(8,128)(2,1)} %param.5, s32[]{:T(128)S(6)} %select_n.89, s32[]{:T(128)S(6)} %select_n.90, s32[]{:T(128)S(6)} %select_n.91), kind=kLoop, calls=%fused_computation.21 | loop fusion | bytes 2097164 | tf_op jit(solution)/shard_map/dynamic_slice | solution.py:160
  1.4 3.1 %collective-permute-start.3 = (bf16[256,2048]{1,0:T(8,128)(2,1)S(1)}, bf16[256,2048]{1,0:T(8,128)(2,1)S(1)}, u32[]{:S(2)}, u32[]{:S(2)}) collective-permute-start(bf16[256,2048]{1,0:T(8,128)(2,1)S(1)} %pad_maximum_fusion.1), channel_id=1, source_target_pairs={{0,4},{4,0},{8,12},{12,8},{16,20},{20,16},{24,28},{28,24},{1,5},{5... | collective-permute-start | bytes 3145736 | tf_op jit(solution)/shard_map/ppermute | solution.py:25
  4.5 2.6 %collective-permute-start = (bf16[1024,128]{1,0:T(8,128)(2,1)}, bf16[1024,128]{1,0:T(8,128)(2,1)}, u32[]{:S(2)}, u32[]{:S(2)}) collective-permute-start(bf16[1024,128]{1,0:T(8,128)(2,1)} %raw_ref.1), channel_id=1, source_target_pairs={{0,16},{4,20},{8,24},{12,28},{16,0},{20,4},{24,8},{28,12},{1,17},{... | collective-permute-start | bytes 786440 | tf_op jit(solution)/shard_map/ppermute | solution.py:25
  7.1 1.2 %broadcast_select_fusion = (f32[256,128]{1,0:T(8,128)S(1)}, f32[256,128]{1,0:T(8,128)S(1)}, f32[256,128]{1,0:T(8,128)S(1)}, f32[256,128]{1,0:T(8,128)}) fusion(pred[]{:T(512)S(6)} %eq.27, f32[128]{0:T(128)S(1)} %get-tuple-element.37, f32[128]{0:T(128)S(1)} %get-tuple-element.38, f32[256]{0:T(256)S(1)} %iota_convert_fusion), kind=kLoop, calls=%fused_computation.5 | loop fusion | flops 131072 | bytes 526337 | tf_op jit(solution)/shard_map/jit(_where)/select_n | solution.py:59
  8.3 19.4 %collective-permute-done.3.first_ref = bf16[256,2048]{1,0:T(8,128)(2,1)S(1)} collective-permute-done((bf16[256,2048]{1,0:T(8,128)(2,1)S(1)}, bf16[256,2048]{1,0:T(8,128)(2,1)S(1)}, u32[]{:S(2)}, u32[]{:S(2)}) %collective-permute-start.3) | collective-permute-done | bytes 1048608 | tf_op jit(solution)/shard_map/ppermute | solution.py:25
  27.6 0.8 %fusion.7 = (bf16[1024,128]{1,0:T(8,128)(2,1)}, bf16[1024,128]{1,0:T(8,128)(2,1)}) fusion(bf16[1024,256]{1,0:T(8,128)(2,1)S(1)} %copy-done.2), kind=kLoop, calls=%fused_computation.22 | loop fusion | bytes 1048576 | tf_op jit(solution)/shard_map/slice | solution.py:166
  28.5 2.8 %collective-permute-start.9 = (bf16[1024,128]{1,0:T(8,128)(2,1)}, bf16[1024,128]{1,0:T(8,128)(2,1)}, u32[]{:S(2)}, u32[]{:S(2)}) collective-permute-start(bf16[1024,128]{1,0:T(8,128)(2,1)} %get-tuple-element.26.raw_ref), channel_id=1, source_target_pairs={{0,16},{4,20},{8,24},{12,28},{16,0},{20,4},{24,8},{28,12},{1,17},{... | collective-permute-start | bytes 786440 | tf_op jit(solution)/shard_map/ppermute | solution.py:25
  31.3 1.7 %constant_dynamic-slice_fusion.1 = (bf16[512,1024]{1,0:T(8,128)(2,1)S(1)}, bf16[512,1024]{1,0:T(8,128)(2,1)S(1)}) fusion(bf16[512,4096]{1,0:T(8,128)(2,1)} %param.5, s32[]{:T(128)S(6)} %select_n.85, s32[]{:T(128)S(6)} %select_n.86), kind=kLoop, calls=%fused_computation.20 | loop fusion | bytes 4194312 | tf_op jit(solution)/shard_map/dynamic_slice | solution.py:162
  33.4 0.3 copy-done.3
  33.7 0.7 dynamic_slice.17
  35.0 1.0 %shard_map.58.mine_ref = bf16[1024,128]{1,0:T(8,128)(2,1)S(1)} custom-call(s32[1]{0:T(128)} %bitcast.2.keep_ref, bf16[1024,128]{1,0:T(8,128)(2,1)} %raw_ref.1, bf16[1024,128]{1,0:T(8,128)(2,1)} %collective-permute-done.other_ref), custom_call_target="tpu_custom_call" | custom-call | bytes 524288 | tf_op jit(solution)/shard_map/pallas_call | solution.py:101
  36.0 1.6 %collective-permute-start.6 = (bf16[1024,128]{1,0:T(8,128)(2,1)S(1)}, bf16[1024,128]{1,0:T(8,128)(2,1)S(1)}, u32[]{:S(2)}, u32[]{:S(2)}) collective-permute-start(bf16[1024,128]{1,0:T(8,128)(2,1)S(1)} %shard_map.58.mine_ref), channel_id=1, source_target_pairs={{0,8},{4,12},{8,0},{12,4},{16,24},{20,28},{24,16},{28,20},{1,9},{5... | collective-permute-start | bytes 786440 | tf_op jit(solution)/shard_map/ppermute | solution.py:25
  37.6 12.5 %collective-permute-done.9.other_ref = bf16[1024,128]{1,0:T(8,128)(2,1)} collective-permute-done((bf16[1024,128]{1,0:T(8,128)(2,1)}, bf16[1024,128]{1,0:T(8,128)(2,1)}, u32[]{:S(2)}, u32[]{:S(2)}) %collective-permute-start.9) | collective-permute-done | bytes 262176 | tf_op jit(solution)/shard_map/ppermute | solution.py:25
  50.1 1.0 %shard_map.62.mine_ref = bf16[1024,128]{1,0:T(8,128)(2,1)S(1)} custom-call(s32[1]{0:T(128)} %bitcast.2.keep_ref, bf16[1024,128]{1,0:T(8,128)(2,1)} %get-tuple-element.26.raw_ref, bf16[1024,128]{1,0:T(8,128)(2,1)} %collective-permute-done.9.other_ref), custom_call_target="tpu_custom_call" | custom-call | bytes 524288 | tf_op jit(solution)/shard_map/pallas_call | solution.py:101
  51.1 0.5 collective-permute-start.10
  51.6 3.9 %collective-permute-done.1.other_ref = bf16[1024,128]{1,0:T(8,128)(2,1)} collective-permute-done((bf16[1024,128]{1,0:T(8,128)(2,1)}, bf16[1024,128]{1,0:T(8,128)(2,1)}, u32[]{:S(2)}, u32[]{:S(2)}) %collective-permute-start.1) | collective-permute-done | bytes 262176 | tf_op jit(solution)/shard_map/ppermute | solution.py:25
  55.5 1.0 %shard_map.55.mine_ref = bf16[1024,128]{1,0:T(8,128)(2,1)S(1)} custom-call(s32[1]{0:T(128)} %bitcast.2.keep_ref, bf16[1024,128]{1,0:T(8,128)(2,1)} %get-tuple-element.19.raw_ref, bf16[1024,128]{1,0:T(8,128)(2,1)} %collective-permute-done.1.other_ref), custom_call_target="tpu_custom_call" | custom-call | bytes 524288 | tf_op jit(solution)/shard_map/pallas_call | solution.py:101
  56.5 0.7 collective-permute-start.2
  57.2 1.9 %shard_map.60 = bf16[512,128]{1,0:T(8,128)(2,1)S(1)} custom-call(s32[1]{0:T(128)} %bitcast.3.core_ref, bf16[256,2048]{1,0:T(8,128)(2,1)S(1)} %collective-permute-done.3.first_ref, bf16[256,2048]{1,0:T(8,128)(2,1)} %collective-permute-done.4.second_ref, bf16[1024,128]{1,0:T(8,128)(2,1)S(1)} %shard_map.58.mine_ref, ...), custom_call_target="tpu_custom_call" | custom-call | flops 268435456 | bytes 1048576 | tf_op jit(solution)/shard_map/pallas_call | solution.py:37
  59.2 1.6 %collective-permute-start.7 = (bf16[512,128]{1,0:T(8,128)(2,1)S(1)}, bf16[512,128]{1,0:T(8,128)(2,1)S(1)}, u32[]{:S(2)}, u32[]{:S(2)}) collective-permute-start(bf16[512,128]{1,0:T(8,128)(2,1)S(1)} %shard_map.60), channel_id=1, source_target_pairs={{0,4},{4,0},{8,12},{12,8},{16,20},{20,16},{24,28},{28,24},{1,5},{5... | collective-permute-start | bytes 393224 | tf_op jit(solution)/shard_map/ppermute | solution.py:25
  60.7 0.7 shard_map.59.own_ref
  61.5 2.0 %shard_map.64 = bf16[512,128]{1,0:T(8,128)(2,1)S(1)} custom-call(s32[1]{0:T(128)} %bitcast.3.core_ref, bf16[256,2048]{1,0:T(8,128)(2,1)S(1)} %collective-permute-done.3.first_ref, bf16[256,2048]{1,0:T(8,128)(2,1)} %collective-permute-done.4.second_ref, bf16[1024,128]{1,0:T(8,128)(2,1)S(1)} %shard_map.62.mine_ref, ...), custom_call_target="tpu_custom_call" | custom-call | flops 268435456 | bytes 1048576 | tf_op jit(solution)/shard_map/pallas_call | solution.py:37
  63.4 1.2 %collective-permute-start.11 = (bf16[512,128]{1,0:T(8,128)(2,1)S(1)}, bf16[512,128]{1,0:T(8,128)(2,1)S(1)}, u32[]{:S(2)}, u32[]{:S(2)}) collective-permute-start(bf16[512,128]{1,0:T(8,128)(2,1)S(1)} %shard_map.64), channel_id=1, source_target_pairs={{0,4},{4,0},{8,12},{12,8},{16,20},{20,16},{24,28},{28,24},{1,5},{5... | collective-permute-start | bytes 393224 | tf_op jit(solution)/shard_map/ppermute | solution.py:25
  64.6 0.2 shard_map.61.kv_ref
  64.9 1.7 %collective-permute-done.2.far_ref = bf16[1024,128]{1,0:T(8,128)(2,1)S(1)} collective-permute-done((bf16[1024,128]{1,0:T(8,128)(2,1)S(1)}, bf16[1024,128]{1,0:T(8,128)(2,1)S(1)}, u32[]{:S(2)}, u32[]{:S(2)}) %collective-permute-start.2) | collective-permute-done | bytes 262176 | tf_op jit(solution)/shard_map/ppermute | solution.py:25
  66.6 1.9 %shard_map.57 = bf16[512,128]{1,0:T(8,128)(2,1)S(1)} custom-call(s32[1]{0:T(128)} %bitcast.3.core_ref, bf16[256,2048]{1,0:T(8,128)(2,1)S(1)} %collective-permute-done.3.first_ref, bf16[256,2048]{1,0:T(8,128)(2,1)} %collective-permute-done.4.second_ref, bf16[1024,128]{1,0:T(8,128)(2,1)S(1)} %shard_map.55.mine_ref, ...), custom_call_target="tpu_custom_call" | custom-call | flops 268435456 | bytes 1048576 | tf_op jit(solution)/shard_map/pallas_call | solution.py:37
  68.5 1.6 %collective-permute-start.5 = (bf16[512,128]{1,0:T(8,128)(2,1)S(1)}, bf16[512,128]{1,0:T(8,128)(2,1)S(1)}, u32[]{:S(2)}, u32[]{:S(2)}) collective-permute-start(bf16[512,128]{1,0:T(8,128)(2,1)S(1)} %shard_map.57), channel_id=1, source_target_pairs={{0,4},{4,0},{8,12},{12,8},{16,20},{20,16},{24,28},{28,24},{1,5},{5... | collective-permute-start | bytes 393224 | tf_op jit(solution)/shard_map/ppermute | solution.py:25
  70.1 0.7 shard_map.63.own_ref
  70.8 0.7 shard_map.56.own_ref
  71.6 2.2 %shard_map.65.refs_0_ = bf16[512,256]{1,0:T(8,128)(2,1)} custom-call(s32[2]{0:T(128)S(1)} %copy-done.1, s32[1]{0:T(128)} %bitcast.even_ref, f32[512,128]{1,0:T(8,128)S(1)} %shard_map.63.own_ref, bf16[512,128]{1,0:T(8,128)(2,1)S(1)} %collective-permute-done.11.sent_ref, f32[256,128]{1,0:T(8,128)S(1)} %get-tuple-element.21.cos_ref, ...), custom_call_target="tpu_custom_call" | custom-call | flops 67108864 | bytes 262144 | tf_op jit(solution)/shard_map/pallas_call | solution.py:37
  73.8 0.2 collective-permute-done.5.sent_ref
  74.0 2.2 %shard_map.66 = bf16[512,256]{1,0:T(8,128)(2,1)} custom-call(s32[2]{0:T(128)S(1)} %copy-done.1, s32[1]{0:T(128)} %bitcast.even_ref, f32[512,128]{1,0:T(8,128)S(1)} %shard_map.56.own_ref, bf16[512,128]{1,0:T(8,128)(2,1)S(1)} %collective-permute-done.5.sent_ref, f32[256,128]{1,0:T(8,128)S(1)} %get-tuple-element.21.cos_ref, ...), custom_call_target="tpu_custom_call", output_to_operand_aliasing={{}: (8, {})} | custom-call | flops 67108864 | bytes 262144 | tf_op jit(solution)/shard_map/pallas_call | solution.py:37
  (21 shorter events, 0.6 us)
Async XLA Ops:
  0.0 27.6 %copy-start.2 = (bf16[1024,256]{1,0:T(8,128)(2,1)S(1)}, bf16[1024,256]{1,0:T(8,128)(2,1)}, u32[]{:S(2)}) copy-start(bf16[1024,256]{1,0:T(8,128)(2,1)} %param.6) | copy-start | bytes 1572868
  1.4 26.2 %collective-permute-start.3 = (bf16[256,2048]{1,0:T(8,128)(2,1)S(1)}, bf16[256,2048]{1,0:T(8,128)(2,1)S(1)}, u32[]{:S(2)}, u32[]{:S(2)}) collective-permute-start(bf16[256,2048]{1,0:T(8,128)(2,1)S(1)} %pad_maximum_fusion.1), channel_id=1, source_target_pairs={{0,4},{4,0},{8,12},{12,8},{16,20},{20,16},{24,28},{28,24},{1,5},{5... | collective-permute-start | bytes 3145736 | tf_op jit(solution)/shard_map/ppermute | solution.py:25
  4.5 28.7 %collective-permute-start = (bf16[1024,128]{1,0:T(8,128)(2,1)}, bf16[1024,128]{1,0:T(8,128)(2,1)}, u32[]{:S(2)}, u32[]{:S(2)}) collective-permute-start(bf16[1024,128]{1,0:T(8,128)(2,1)} %raw_ref.1), channel_id=1, source_target_pairs={{0,16},{4,20},{8,24},{12,28},{16,0},{20,4},{24,8},{28,12},{1,17},{... | collective-permute-start | bytes 786440 | tf_op jit(solution)/shard_map/ppermute | solution.py:25
  27.6 29.6 %collective-permute-start.4 = (bf16[256,2048]{1,0:T(8,128)(2,1)S(1)}, bf16[256,2048]{1,0:T(8,128)(2,1)}, u32[]{:S(2)}, u32[]{:S(2)}) collective-permute-start(bf16[256,2048]{1,0:T(8,128)(2,1)S(1)} %collective-permute-done.3.first_ref), channel_id=1, source_target_pairs={{0,1},{1,0},{2,3},{3,2},{4,5},{5,4},{6,7},{7,6},{8,9},{9,8},{10,11... | collective-permute-start | bytes 3145736 | tf_op jit(solution)/shard_map/ppermute | solution.py:25
  28.5 21.6 %collective-permute-start.9 = (bf16[1024,128]{1,0:T(8,128)(2,1)}, bf16[1024,128]{1,0:T(8,128)(2,1)}, u32[]{:S(2)}, u32[]{:S(2)}) collective-permute-start(bf16[1024,128]{1,0:T(8,128)(2,1)} %get-tuple-element.26.raw_ref), channel_id=1, source_target_pairs={{0,16},{4,20},{8,24},{12,28},{16,0},{20,4},{24,8},{28,12},{1,17},{... | collective-permute-start | bytes 786440 | tf_op jit(solution)/shard_map/ppermute | solution.py:25
  33.0 0.7 copy-start.3
  33.2 22.3 %collective-permute-start.1 = (bf16[1024,128]{1,0:T(8,128)(2,1)}, bf16[1024,128]{1,0:T(8,128)(2,1)}, u32[]{:S(2)}, u32[]{:S(2)}) collective-permute-start(bf16[1024,128]{1,0:T(8,128)(2,1)} %get-tuple-element.19.raw_ref), channel_id=1, source_target_pairs={{0,16},{4,20},{8,24},{12,28},{16,0},{20,4},{24,8},{28,12},{1,17},{... | collective-permute-start | bytes 786440 | tf_op jit(solution)/shard_map/ppermute | solution.py:25
  36.0 21.2 %collective-permute-start.6 = (bf16[1024,128]{1,0:T(8,128)(2,1)S(1)}, bf16[1024,128]{1,0:T(8,128)(2,1)S(1)}, u32[]{:S(2)}, u32[]{:S(2)}) collective-permute-start(bf16[1024,128]{1,0:T(8,128)(2,1)S(1)} %shard_map.58.mine_ref), channel_id=1, source_target_pairs={{0,8},{4,12},{8,0},{12,4},{16,24},{20,28},{24,16},{28,20},{1,9},{5... | collective-permute-start | bytes 786440 | tf_op jit(solution)/shard_map/ppermute | solution.py:25
  51.1 10.4 %collective-permute-start.10 = (bf16[1024,128]{1,0:T(8,128)(2,1)S(1)}, bf16[1024,128]{1,0:T(8,128)(2,1)S(1)}, u32[]{:S(2)}, u32[]{:S(2)}) collective-permute-start(bf16[1024,128]{1,0:T(8,128)(2,1)S(1)} %shard_map.62.mine_ref), channel_id=1, source_target_pairs={{0,8},{4,12},{8,0},{12,4},{16,24},{20,28},{24,16},{28,20},{1,9},{5... | collective-permute-start | bytes 786440 | tf_op jit(solution)/shard_map/ppermute | solution.py:25
  56.5 10.1 %collective-permute-start.2 = (bf16[1024,128]{1,0:T(8,128)(2,1)S(1)}, bf16[1024,128]{1,0:T(8,128)(2,1)S(1)}, u32[]{:S(2)}, u32[]{:S(2)}) collective-permute-start(bf16[1024,128]{1,0:T(8,128)(2,1)S(1)} %shard_map.55.mine_ref), channel_id=1, source_target_pairs={{0,8},{4,12},{8,0},{12,4},{16,24},{20,28},{24,16},{28,20},{1,9},{5... | collective-permute-start | bytes 786440 | tf_op jit(solution)/shard_map/ppermute | solution.py:25
  59.2 5.4 %collective-permute-start.7 = (bf16[512,128]{1,0:T(8,128)(2,1)S(1)}, bf16[512,128]{1,0:T(8,128)(2,1)S(1)}, u32[]{:S(2)}, u32[]{:S(2)}) collective-permute-start(bf16[512,128]{1,0:T(8,128)(2,1)S(1)} %shard_map.60), channel_id=1, source_target_pairs={{0,4},{4,0},{8,12},{12,8},{16,20},{20,16},{24,28},{28,24},{1,5},{5... | collective-permute-start | bytes 393224 | tf_op jit(solution)/shard_map/ppermute | solution.py:25
  61.5 3.1 %copy-start = (f32[256,128]{1,0:T(8,128)S(1)}, f32[256,128]{1,0:T(8,128)}, u32[]{:S(2)}) copy-start(f32[256,128]{1,0:T(8,128)} %get-tuple-element.24.cos_ref) | copy-start | bytes 393220
  63.4 8.1 %collective-permute-start.11 = (bf16[512,128]{1,0:T(8,128)(2,1)S(1)}, bf16[512,128]{1,0:T(8,128)(2,1)S(1)}, u32[]{:S(2)}, u32[]{:S(2)}) collective-permute-start(bf16[512,128]{1,0:T(8,128)(2,1)S(1)} %shard_map.64), channel_id=1, source_target_pairs={{0,4},{4,0},{8,12},{12,8},{16,20},{20,16},{24,28},{28,24},{1,5},{5... | collective-permute-start | bytes 393224 | tf_op jit(solution)/shard_map/ppermute | solution.py:25
  64.8 6.8 %collective-permute-start.8 = (bf16[512,128]{1,0:T(8,128)(2,1)S(1)}, bf16[512,128]{1,0:T(8,128)(2,1)S(1)}, u32[]{:S(2)}, u32[]{:S(2)}) collective-permute-start(bf16[512,128]{1,0:T(8,128)(2,1)S(1)} %shard_map.61.kv_ref), channel_id=1, source_target_pairs={{0,1},{1,0},{2,3},{3,2},{4,5},{5,4},{6,7},{7,6},{8,9},{9,8},{10,11... | collective-permute-start | bytes 393224 | tf_op jit(solution)/shard_map/ppermute | solution.py:25
  68.5 5.5 %collective-permute-start.5 = (bf16[512,128]{1,0:T(8,128)(2,1)S(1)}, bf16[512,128]{1,0:T(8,128)(2,1)S(1)}, u32[]{:S(2)}, u32[]{:S(2)}) collective-permute-start(bf16[512,128]{1,0:T(8,128)(2,1)S(1)} %shard_map.57), channel_id=1, source_target_pairs={{0,4},{4,0},{8,12},{12,8},{16,20},{20,16},{24,28},{28,24},{1,5},{5... | collective-permute-start | bytes 393224 | tf_op jit(solution)/shard_map/ppermute | solution.py:25
  70.8 0.7 copy-start.1

commit v3 on v2

--- a/solution.py
+++ b/solution.py
@@ -12,7 +12,6 @@
 HEAD_DIM = 128
 SEQ_LEN = 256
 OLD_DATA = 4
-IN_FLIGHT = 2
 
 
 VMEM = pl.BlockSpec(memory_space=pltpu.VMEM)
@@ -33,18 +32,16 @@
     return jnp.dot(left, right, preferred_element_type=jnp.float32)
 
 
-def call(kernel, scalars, operands, outs, cost, out_specs=VMEM, spare=(), **more):
+def call(kernel, scalars, operands, outs, cost, out_specs=VMEM, **more):
     return pl.pallas_call(
         kernel,
         out_shape=outs,
-        in_specs=[SMEM] * len(scalars)
-        + [VMEM] * len(operands)
-        + [pl.BlockSpec(memory_space=pltpu.HBM)] * len(spare),
+        in_specs=[SMEM] * len(scalars) + [VMEM] * len(operands),
         out_specs=jax.tree.map(lambda _: out_specs, outs),
         compiler_params=pltpu.CompilerParams(vmem_limit_bytes=8 * 2**20),
         cost_estimate=pl.CostEstimate(flops=cost, bytes_accessed=cost // 256, transcendentals=0),
         **more,
-    )(*scalars, *operands, *spare)
+    )(*scalars, *operands)
 
 
 def tables(turned):
@@ -61,17 +58,14 @@
 
 def turn(values, cosine, sine):
     lanes = lax.broadcasted_iota(jnp.int32, values.shape, 1)
-    swapped = jnp.where(
-        lanes % 2 == 0,
-        pltpu.roll(values, values.shape[1] - 1, axis=1),
-        pltpu.roll(values, 1, axis=1),
-    )
+    swapped = jnp.take_along_axis(values, lanes ^ 1, axis=1, mode="promise_in_bounds")
     return values * cosine + swapped * sine
 
 
 def attend_head(queries, keys, values, length):
     half = SEQ_LEN // 2
     scale = math.log2(math.e) / math.sqrt(HEAD_DIM)
+    values = jnp.concatenate([values, jnp.ones_like(values)], axis=1)
     parts = []
     for start, stop in ((0, half), (half, SEQ_LEN)):
         rows = start + lax.broadcasted_iota(jnp.int32, (stop - start, stop), 0)
@@ -81,9 +75,9 @@
         )
         scores = jnp.where((spots <= rows) & (spots < length), scores, -1e30)
         top = jnp.max(scores, axis=-1, keepdims=True)
-        raised = jnp.exp2((scores - top) * scale)
-        total = jnp.sum(raised, axis=-1, keepdims=True)
-        parts.append(dot(raised.astype(jnp.bfloat16), values[:stop]) / total)
+        raised = jnp.exp2((scores - top) * scale).astype(jnp.bfloat16)
+        mixed = dot(raised, values[:stop])
+        parts.append(mixed[:, :HEAD_DIM] / mixed[:, HEAD_DIM:])
     return jnp.concatenate(parts, axis=0)
 
 
@@ -114,12 +108,15 @@
     out_ref[...] = dot(own_ref[:, :depth], mine_ref[...]) + dot(own_ref[:, depth:], far_ref[...])
 
 
-def their_kernel(core_ref, first_ref, second_ref, mine_ref, far_ref, out_ref):
-    half, depth = first_ref.shape[0], mine_ref.shape[0]
-    mine, far = mine_ref[...], far_ref[...]
+def their_kernel(start, core_ref, first_ref, second_ref, block_ref, *refs):
+    out_ref, half, depth = refs[-1], first_ref.shape[0], block_ref.shape[0]
+    block = block_ref[...]
     for which, ref in ((core_ref[0], first_ref), (1 - core_ref[0], second_ref)):
-        total = dot(ref[:, :depth], mine) + dot(ref[:, depth:], far)
-        out_ref[pl.ds(pl.multiple_of(which * half, half), half), :] = total.astype(out_ref.dtype)
+        at = pl.ds(pl.multiple_of(which * half, half), half)
+        total = dot(ref[:, start : start + depth], block)
+        if len(refs) > 1:
+            total += refs[0][at, :]
+        out_ref[at, :] = total.astype(out_ref.dtype)
 
 
 def finish_kernel(own_ref, sent_ref, cos_ref, sin_ref, out_ref):
@@ -129,21 +126,31 @@
         out_ref[cut, :] = turn(total, cos_ref[...], sin_ref[...]).astype(out_ref.dtype)
 
 
-def head_kernel(head, lengths_ref, even_ref, own_ref, sent_ref, cos_ref, sin_ref, kv_ref, partner_ref, *refs):
-    is_even = even_ref[0] == 1
-    out_ref, held, sems = refs[-3:]
-    columns = slice(head * HEAD_DIM, (head + 1) * HEAD_DIM)
+def head_kernel(facts_ref, own_ref, sent_ref, cos_ref, sin_ref, kv_ref, partner_ref, *refs):
+    seqs = own_ref.shape[0] // SEQ_LEN
+    is_even = facts_ref[seqs] == 1
+    last = len(refs) > 1
+    done_refs, held = refs[:-3], refs[-2] if last else refs[0]
     copies = []
-    for seq in range(own_ref.shape[0] // SEQ_LEN):
+
+    def send(ref, head, cut):
+        if last:
+            columns = slice(head * HEAD_DIM, (head + 1) * HEAD_DIM)
+            copy = pltpu.make_async_copy(ref.at[cut, :], refs[-3].at[cut, columns], refs[-1].at[len(copies)])
+            copies.append(copy)
+            copy.start()
+
+    for head, ref in enumerate(done_refs):
+        send(ref, head, slice(0, ref.shape[0]))
+    for seq in range(seqs):
         cut = slice(seq * SEQ_LEN, (seq + 1) * SEQ_LEN)
         total = own_ref[cut, :] + sent_ref[cut, :].astype(jnp.float32)
         queries = turn(total, cos_ref[...], sin_ref[...]).astype(jnp.bfloat16)
         mine, partner = kv_ref[cut, :], partner_ref[cut, :]
         keys = jnp.where(is_even, mine, partner)
         values = jnp.where(is_even, partner, mine)
-        held[cut, :] = attend_head(queries, keys, values, lengths_ref[seq]).astype(held.dtype)
-        copies.append(pltpu.make_async_copy(held.at[cut, :], out_ref.at[cut, columns], sems.at[seq]))
-        copies[-1].start()
+        held[cut, :] = attend_head(queries, keys, values, facts_ref[seq]).astype(held.dtype)
+        send(held, len(done_refs), cut)
     for copy in copies:
         copy.wait()
 
@@ -167,12 +174,17 @@
     blocks = [kv_weight, *after(tuple(columns))]
     others = []
     for index, raw in enumerate(blocks):
-        if index >= IN_FLIGHT:
+        if index == 1:
+            raw, staged = after((raw, choose(jnp.ones((1,), jnp.int32), kv_weight, kv_weight)))
+            blocks[0] = staged
+        if index:
+            raw, others[0] = after((raw, others[0]))
+        if index > 1:
             raw, own_part = after((raw, own_part))
-            raw, others[index - IN_FLIGHT] = after((raw, others[index - IN_FLIGHT]))
         blocks[index] = raw
         others.append(swapped(raw, "dp", OLD_DATA))
     even = (core == 0).astype(jnp.int32).reshape(1)
+    facts = jnp.concatenate([lengths, even])
     core = core.astype(jnp.int32).reshape(1)
     keep = keep.astype(jnp.int32).reshape(1)
     first, turns = after((first, tables(even[0] == 1)))
@@ -183,15 +195,27 @@
         mine = choose(keep, raw, other)
         settled.append((mine, swapped(mine, "dp", 2)))
 
-    own_kv = partner = result = None
-    work = 4 * tokens * depth * HEAD_DIM
+    sums, dots = [], 4 * tokens * depth * HEAD_DIM
     for index, (mine, far) in enumerate(settled):
+        if index > 1:
+            own, back = sums[-1]
+            far, own = after((far, own))
+            sums[-1] = (own, back)
         theirs = call(
-            their_kernel,
+            functools.partial(their_kernel, 0),
             [core],
-            [near(value) for value in (first, second, mine, far)],
-            pltpu.VMEM((tokens, HEAD_DIM), jnp.bfloat16),
-            work,
+            [near(value) for value in (first, second, mine)],
+            pltpu.VMEM((tokens, HEAD_DIM), jnp.float32),
+            dots // 2,
+        )
+        if index > 1:
+            far, theirs = after((far, theirs))
+        theirs = call(
+            functools.partial(their_kernel, depth),
+            [core],
+            [near(value) for value in (first, second, far, theirs)],
+            pltpu.VMEM((tokens, HEAD_DIM), jnp.float32 if index < 2 else jnp.bfloat16),
+            dots // 2,
         )
         back = swapped(theirs, "dp", 1)
         own = call(
@@ -199,8 +223,9 @@
             [],
             [near(value) for value in (own_part, mine, far)],
             pltpu.VMEM((tokens, HEAD_DIM), jnp.float32),
-            work,
+            dots,
         )
+        sums.append((own, back))
         if index == 0:
             own_kv = call(
                 finish_kernel,
@@ -210,23 +235,22 @@
                 tokens * HEAD_DIM * 8,
             )
             partner = swapped(own_kv, "tensor", 1)
-            continue
-        head = index - 1
-        result = call(
-            functools.partial(head_kernel, head),
-            [lengths, even],
-            [near(value) for value in (own, back, cosine, sine, own_kv, partner)],
-            jax.ShapeDtypeStruct((tokens, heads * HEAD_DIM), jnp.bfloat16),
-            tokens * SEQ_LEN * HEAD_DIM * 4,
-            out_specs=pl.BlockSpec(memory_space=pltpu.HBM),
-            scratch_shapes=[
-                pltpu.VMEM((tokens, HEAD_DIM), jnp.bfloat16),
-                pltpu.SemaphoreType.DMA((tokens // SEQ_LEN,)),
-            ],
-            spare=[] if result is None else [result],
-            input_output_aliases={} if result is None else {8: 0},
-        )
-    return result
+
+    done, work = [], tokens * SEQ_LEN * HEAD_DIM * 4
+    held = pltpu.VMEM((tokens, HEAD_DIM), jnp.bfloat16)
+    for own, back in sums[1:-1]:
+        operands = [near(value) for value in (own, back, cosine, sine, own_kv, partner)]
+        done.append(call(head_kernel, [facts], operands, held, work))
+    own, back = sums[-1]
+    return call(
+        head_kernel,
+        [facts],
+        [near(value) for value in (own, back, cosine, sine, own_kv, partner, *done)],
+        jax.ShapeDtypeStruct((tokens, heads * HEAD_DIM), jnp.bfloat16),
+        work,
+        out_specs=pl.BlockSpec(memory_space=pltpu.HBM),
+        scratch_shapes=[held, pltpu.SemaphoreType.DMA((len(done) + tokens // SEQ_LEN,))],
+    )
 
 
 def many_sections(hidden, q_weight, kv_weight, owner, lengths):

time: 76.5 us -> 88.9 us (1.16)
  waiting for transfers between devices: 37.6 us -> 56.3 us
  Pallas kernels: 15.3 us -> 10 us
  starting transfers between devices: 16 us -> 13.7 us
  other arithmetic: 1.48 us -> 2.91 us
    ppermute x12, waiting for transfers between devices: 37.6 us -> 56.3 us  [swapped(): return lax.ppermute(value, axis, pairs)]
    pallas_call x9 -> x12, Pallas kernels: 12.5 us -> 8.04 us  [call(): pl.pallas_call(kernel, out_shape=outs, in_specs=[SMEM] * len(scalars) + [...]
    ppermute x12, starting transfers between devices: 16 us -> 13.7 us  [swapped(): return lax.ppermute(value, axis, pairs)]
    concatenate x1, other arithmetic: 0.18 us -> 1.52 us  [two_sections(): own_part = jnp.concatenate([whole(quarter), whole(quarter ^ 2)], axis=1)]
    pallas_call x3 -> x4, Pallas kernels: 2.88 us -> 2 us  [choose(): pl.pallas_call(choose_kernel, out_shape=pltpu.VMEM(raw.shape, raw.dtype),...]
  transfers between devices with their start and end apart: 12 -> 12, of which waited for: 5 -> 9; matrix products, arithmetic and copies ran while one was open for 6% -> 7% of each run, Pallas kernels for 17% -> 9%
where the time goes in v3:
time: 88.9 us; the launch traced here: 88.6 us
  waiting for transfers between devices  56.3 us (63%)
  starting transfers between devices  13.7 us (15%)
  Pallas kernels  10 us (11%)
  local copies, waits for them, and re-layouts  4.76 us (5%)
  other arithmetic  2.91 us (3%)
    ppermute x12, waiting for transfers between devices, swapped(): return lax.ppermute(value, axis, pairs)  56.3 us
    ppermute x12, starting transfers between devices, swapped(): return lax.ppermute(value, axis, pairs)  13.7 us
    pallas_call x12, Pallas kernels, call(): pl.pallas_call(kernel, out_shape=outs, in_specs=[SMEM] * len(scalars) + [...  8.04 us
    pallas_call x4, Pallas kernels, choose(): pl.pallas_call(choose_kernel, out_shape=pltpu.VMEM(raw.shape, raw.dtype),...  2 us
  transfers between devices with their start and end apart: 12, of which 9 were waited for; matrix products, arithmetic and copies ran while one was open for 7% of the time, Pallas kernels for 9%

profile of v3, /device:TPU:0, one launch (start us, length us, event | category | flops | bytes accessed | tf_op | source)
XLA Modules:
  0.0 88.6 jit_solution(8705944792678687046)
XLA Ops:
  0.0 1.3 %fusion.6 = (bf16[256,1024]{1,0:T(8,128)(2,1)S(1)}, bf16[256,1024]{1,0:T(8,128)(2,1)S(1)}) fusion(bf16[512,4096]{1,0:T(8,128)(2,1)} %param.5, s32[]{:T(128)S(6)} %select_n.89, s32[]{:T(128)S(6)} %select_n.90, s32[]{:T(128)S(6)} %select_n.91), kind=kLoop, calls=%fused_computation.22 | loop fusion | bytes 2097164 | tf_op jit(solution)/shard_map/dynamic_slice | solution.py:167
  1.4 3.1 %collective-permute-start.5 = (bf16[256,2048]{1,0:T(8,128)(2,1)S(1)}, bf16[256,2048]{1,0:T(8,128)(2,1)S(1)}, u32[]{:S(2)}, u32[]{:S(2)}) collective-permute-start(bf16[256,2048]{1,0:T(8,128)(2,1)S(1)} %pad_maximum_fusion.1), channel_id=1, source_target_pairs={{0,4},{4,0},{8,12},{12,8},{16,20},{20,16},{24,28},{28,24},{1,5},{5... | collective-permute-start | bytes 3145736 | tf_op jit(solution)/shard_map/ppermute | solution.py:24
  4.5 1.2 %broadcast_select_fusion = (f32[256,128]{1,0:T(8,128)S(1)}, f32[256,128]{1,0:T(8,128)S(1)}, f32[256,128]{1,0:T(8,128)S(1)}, f32[256,128]{1,0:T(8,128)}) fusion(pred[]{:T(512)S(6)} %eq.27, f32[128]{0:T(128)S(1)} %get-tuple-element.53, f32[128]{0:T(128)S(1)} %get-tuple-element.54, f32[256]{0:T(256)S(1)} %iota_convert_fusion), kind=kLoop, calls=%fused_computation.5 | loop fusion | flops 131072 | bytes 526337 | tf_op jit(solution)/shard_map/jit(_where)/select_n | solution.py:56
  5.7 21.9 %collective-permute-done.5.first_ref = bf16[256,2048]{1,0:T(8,128)(2,1)S(1)} collective-permute-done((bf16[256,2048]{1,0:T(8,128)(2,1)S(1)}, bf16[256,2048]{1,0:T(8,128)(2,1)S(1)}, u32[]{:S(2)}, u32[]{:S(2)}) %collective-permute-start.5) | collective-permute-done | bytes 1048608 | tf_op jit(solution)/shard_map/ppermute | solution.py:24
  27.6 2.8 %collective-permute-start = (bf16[1024,128]{1,0:T(8,128)(2,1)S(1)}, bf16[1024,128]{1,0:T(8,128)(2,1)}, u32[]{:S(2)}, u32[]{:S(2)}) collective-permute-start(bf16[1024,128]{1,0:T(8,128)(2,1)S(1)} %copy-done.1), channel_id=1, source_target_pairs={{0,16},{4,20},{8,24},{12,28},{16,0},{20,4},{24,8},{28,12},{1,17},{... | collective-permute-start | bytes 786440 | tf_op jit(solution)/shard_map/ppermute | solution.py:24
  30.4 1.1 %fusion.7 = (bf16[1024,128]{1,0:T(8,128)(2,1)S(1)}, bf16[1024,128]{1,0:T(8,128)(2,1)S(1)}) fusion(bf16[1024,256]{1,0:T(8,128)(2,1)} %param.6), kind=kLoop, calls=%fused_computation.23 | loop fusion | bytes 1048576 | tf_op jit(solution)/shard_map/slice | solution.py:173
  31.6 1.7 %constant_dynamic-slice_fusion.1 = (bf16[512,1024]{1,0:T(8,128)(2,1)S(1)}, bf16[512,1024]{1,0:T(8,128)(2,1)S(1)}) fusion(bf16[512,4096]{1,0:T(8,128)(2,1)} %param.5, s32[]{:T(128)S(6)} %select_n.85, s32[]{:T(128)S(6)} %select_n.86), kind=kLoop, calls=%fused_computation.21 | loop fusion | bytes 4194312 | tf_op jit(solution)/shard_map/dynamic_slice | solution.py:169
  33.3 9.8 %collective-permute-done.other_ref = bf16[1024,128]{1,0:T(8,128)(2,1)} collective-permute-done((bf16[1024,128]{1,0:T(8,128)(2,1)S(1)}, bf16[1024,128]{1,0:T(8,128)(2,1)}, u32[]{:S(2)}, u32[]{:S(2)}) %collective-permute-start) | collective-permute-done | bytes 262176 | tf_op jit(solution)/shard_map/ppermute | solution.py:24
  43.1 1.5 %pad_maximum_fusion.own_ref = bf16[512,2048]{1,0:T(8,128)(2,1)} fusion(bf16[512,1024]{1,0:T(8,128)(2,1)S(1)} %get-tuple-element.46, bf16[512,1024]{1,0:T(8,128)(2,1)S(1)} %get-tuple-element.45), kind=kLoop, calls=%fused_computation | loop fusion | flops 4194304 | bytes 4194304 | tf_op jit(solution)/shard_map/concatenate | solution.py:170
  44.7 2.9 %collective-permute-start.1 = (bf16[1024,128]{1,0:T(8,128)(2,1)S(1)}, bf16[1024,128]{1,0:T(8,128)(2,1)}, u32[]{:S(2)}, u32[]{:S(2)}) collective-permute-start(bf16[1024,128]{1,0:T(8,128)(2,1)S(1)} %get-tuple-element.30.raw_ref), channel_id=1, source_target_pairs={{0,16},{4,20},{8,24},{12,28},{16,0},{20,4},{24,8},{28,12},{1,17},{... | collective-permute-start | bytes 786440 | tf_op jit(solution)/shard_map/ppermute | solution.py:24
  47.6 0.6 dynamic_slice.17
  48.9 1.0 %shard_map.62.mine_ref.block_ref = bf16[1024,128]{1,0:T(8,128)(2,1)S(1)} custom-call(s32[1]{0:T(128)} %bitcast.2.keep_ref, bf16[1024,128]{1,0:T(8,128)(2,1)S(1)} %shard_map.55.raw_ref, bf16[1024,128]{1,0:T(8,128)(2,1)} %collective-permute-done.other_ref), custom_call_target="tpu_custom_call" | custom-call | bytes 524288 | tf_op jit(solution)/shard_map/pallas_call | solution.py:95
  49.8 1.2 %collective-permute-start.8 = (bf16[1024,128]{1,0:T(8,128)(2,1)S(1)}, bf16[1024,128]{1,0:T(8,128)(2,1)S(1)}, u32[]{:S(2)}, u32[]{:S(2)}) collective-permute-start(bf16[1024,128]{1,0:T(8,128)(2,1)S(1)} %shard_map.62.mine_ref.block_ref), channel_id=1, source_target_pairs={{0,8},{4,12},{8,0},{12,4},{16,24},{20,28},{24,16},{28,20},{1,9},{5... | collective-permute-start | bytes 786440 | tf_op jit(solution)/shard_map/ppermute | solution.py:24
  51.1 13.4 %collective-permute-done.3.other_ref = bf16[1024,128]{1,0:T(8,128)(2,1)S(1)} collective-permute-done((bf16[1024,128]{1,0:T(8,128)(2,1)S(1)}, bf16[1024,128]{1,0:T(8,128)(2,1)S(1)}, u32[]{:S(2)}, u32[]{:S(2)}) %collective-permute-start.3) | collective-permute-done | bytes 262176 | tf_op jit(solution)/shard_map/ppermute | solution.py:24
  64.6 4.6 %collective-permute-done.1.other_ref = bf16[1024,128]{1,0:T(8,128)(2,1)} collective-permute-done((bf16[1024,128]{1,0:T(8,128)(2,1)S(1)}, bf16[1024,128]{1,0:T(8,128)(2,1)}, u32[]{:S(2)}, u32[]{:S(2)}) %collective-permute-start.1) | collective-permute-done | bytes 262176 | tf_op jit(solution)/shard_map/ppermute | solution.py:24
  69.1 1.0 %shard_map.56.block_ref.mine_ref = bf16[1024,128]{1,0:T(8,128)(2,1)S(1)} custom-call(s32[1]{0:T(128)} %bitcast.2.keep_ref, bf16[1024,128]{1,0:T(8,128)(2,1)S(1)} %get-tuple-element.30.raw_ref, bf16[1024,128]{1,0:T(8,128)(2,1)} %collective-permute-done.1.other_ref), custom_call_target="tpu_custom_call" | custom-call | bytes 524288 | tf_op jit(solution)/shard_map/pallas_call | solution.py:95
  70.2 0.4 shard_map.64.refs_0_
  70.6 0.4 shard_map.65
  71.1 0.5 collective-permute-start.9
  72.0 2.6 %collective-permute-done.4.far_ref.block_ref = bf16[1024,128]{1,0:T(8,128)(2,1)S(1)} collective-permute-done((bf16[1024,128]{1,0:T(8,128)(2,1)S(1)}, bf16[1024,128]{1,0:T(8,128)(2,1)S(1)}, u32[]{:S(2)}, u32[]{:S(2)}) %collective-permute-start.4) | collective-permute-done | bytes 262176 | tf_op jit(solution)/shard_map/ppermute | solution.py:24
  75.1 1.5 %collective-permute-start.11 = (f32[512,128]{1,0:T(8,128)S(1)}, f32[512,128]{1,0:T(8,128)S(1)}, u32[]{:S(2)}, u32[]{:S(2)}) collective-permute-start(f32[512,128]{1,0:T(8,128)S(1)} %shard_map.68), channel_id=1, source_target_pairs={{0,4},{4,0},{8,12},{12,8},{16,20},{20,16},{24,28},{28,24},{1,5},{5... | collective-permute-start | bytes 786440 | tf_op jit(solution)/shard_map/ppermute | solution.py:24
  76.5 0.7 shard_map.63.own_ref
  77.3 0.7 shard_map.58.own_ref
  78.0 2.2 %collective-permute-done.2.far_ref.block_ref = bf16[1024,128]{1,0:T(8,128)(2,1)S(1)} collective-permute-done((bf16[1024,128]{1,0:T(8,128)(2,1)S(1)}, bf16[1024,128]{1,0:T(8,128)(2,1)S(1)}, u32[]{:S(2)}, u32[]{:S(2)}) %collective-permute-start.2) | collective-permute-done | bytes 262176 | tf_op jit(solution)/shard_map/ppermute | solution.py:24
  80.2 0.4 shard_map.59.refs_0_
  80.6 0.4 shard_map.61
  81.0 1.5 %collective-permute-start.7 = (bf16[512,128]{1,0:T(8,128)(2,1)S(1)}, bf16[512,128]{1,0:T(8,128)(2,1)S(1)}, u32[]{:S(2)}, u32[]{:S(2)}) collective-permute-start(bf16[512,128]{1,0:T(8,128)(2,1)S(1)} %shard_map.61), channel_id=1, source_target_pairs={{0,4},{4,0},{8,12},{12,8},{16,20},{20,16},{24,28},{28,24},{1,5},{5... | collective-permute-start | bytes 393224 | tf_op jit(solution)/shard_map/ppermute | solution.py:24
  82.8 0.7 shard_map.60.own_ref
  83.5 0.5 collective-permute-done.11.sent_ref
  84.1 1.3 %shard_map.69.refs_0_ = bf16[512,128]{1,0:T(8,128)(2,1)S(1)} custom-call(s32[3]{0:T(128)S(1)} %pad_add_fusion.facts_ref, f32[512,128]{1,0:T(8,128)S(1)} %shard_map.58.own_ref, f32[512,128]{1,0:T(8,128)S(1)} %collective-permute-done.11.sent_ref, f32[256,128]{1,0:T(8,128)S(1)} %get-tuple-element.36.cos_ref, f32[256,128]{1,0:T(8,128)S(1)} %get-tuple-element.37.sin_ref, ...), custom_call_target="tpu_custom_call" | custom-call | flops 67108864 | bytes 262144 | tf_op jit(solution)/shard_map/pallas_call | solution.py:36
  85.4 1.3 %collective-permute-done.7.sent_ref = bf16[512,128]{1,0:T(8,128)(2,1)S(1)} collective-permute-done((bf16[512,128]{1,0:T(8,128)(2,1)S(1)}, bf16[512,128]{1,0:T(8,128)(2,1)S(1)}, u32[]{:S(2)}, u32[]{:S(2)}) %collective-permute-start.7) | collective-permute-done | bytes 131104 | tf_op jit(solution)/shard_map/ppermute | solution.py:24
  86.7 1.9 %shard_map.70 = bf16[512,256]{1,0:T(8,128)(2,1)} custom-call(s32[3]{0:T(128)S(1)} %pad_add_fusion.facts_ref, f32[512,128]{1,0:T(8,128)S(1)} %shard_map.60.own_ref, bf16[512,128]{1,0:T(8,128)(2,1)S(1)} %collective-permute-done.7.sent_ref, f32[256,128]{1,0:T(8,128)S(1)} %get-tuple-element.36.cos_ref, f32[256,128]{1,0:T(8,128)S(1)} %get-tuple-element.37.sin_ref, ...), custom_call_target="tpu_custom_call" | custom-call | flops 67108864 | bytes 262144 | tf_op jit(solution)/shard_map/pallas_call | solution.py:36
  (28 shorter events, 1.5 us)
Async XLA Ops:
  0.0 27.6 %copy-start.1 = (bf16[1024,128]{1,0:T(8,128)(2,1)S(1)}, bf16[1024,128]{1,0:T(8,128)(2,1)}, u32[]{:S(2)}) copy-start(bf16[1024,128]{1,0:T(8,128)(2,1)} %other_ref.1) | copy-start | bytes 786436
  1.4 26.2 %collective-permute-start.5 = (bf16[256,2048]{1,0:T(8,128)(2,1)S(1)}, bf16[256,2048]{1,0:T(8,128)(2,1)S(1)}, u32[]{:S(2)}, u32[]{:S(2)}) collective-permute-start(bf16[256,2048]{1,0:T(8,128)(2,1)S(1)} %pad_maximum_fusion.1), channel_id=1, source_target_pairs={{0,4},{4,0},{8,12},{12,8},{16,20},{20,16},{24,28},{28,24},{1,5},{5... | collective-permute-start | bytes 3145736 | tf_op jit(solution)/shard_map/ppermute | solution.py:24
  27.6 42.5 %collective-permute-start.6 = (bf16[256,2048]{1,0:T(8,128)(2,1)S(1)}, bf16[256,2048]{1,0:T(8,128)(2,1)S(1)}, u32[]{:S(2)}, u32[]{:S(2)}) collective-permute-start(bf16[256,2048]{1,0:T(8,128)(2,1)S(1)} %collective-permute-done.5.first_ref), channel_id=1, source_target_pairs={{0,1},{1,0},{2,3},{3,2},{4,5},{5,4},{6,7},{7,6},{8,9},{9,8},{10,11... | collective-permute-start | bytes 3145736 | tf_op jit(solution)/shard_map/ppermute | solution.py:24
  27.6 15.5 %collective-permute-start = (bf16[1024,128]{1,0:T(8,128)(2,1)S(1)}, bf16[1024,128]{1,0:T(8,128)(2,1)}, u32[]{:S(2)}, u32[]{:S(2)}) collective-permute-start(bf16[1024,128]{1,0:T(8,128)(2,1)S(1)} %copy-done.1), channel_id=1, source_target_pairs={{0,16},{4,20},{8,24},{12,28},{16,0},{20,4},{24,8},{28,12},{1,17},{... | collective-permute-start | bytes 786440 | tf_op jit(solution)/shard_map/ppermute | solution.py:24
  43.1 21.3 %collective-permute-start.3 = (bf16[1024,128]{1,0:T(8,128)(2,1)S(1)}, bf16[1024,128]{1,0:T(8,128)(2,1)S(1)}, u32[]{:S(2)}, u32[]{:S(2)}) collective-permute-start(bf16[1024,128]{1,0:T(8,128)(2,1)S(1)} %get-tuple-element.31.raw_ref), channel_id=1, source_target_pairs={{0,16},{4,20},{8,24},{12,28},{16,0},{20,4},{24,8},{28,12},{1,17},{... | collective-permute-start | bytes 786440 | tf_op jit(solution)/shard_map/ppermute | solution.py:24
  43.1 4.4 %copy-start.3 = (s32[4]{0:T(128)S(1)}, s32[4]{0:T(128)}, u32[]{:S(2)}) copy-start(s32[4]{0:T(128)} %param.8) | copy-start | bytes 52
  44.7 24.5 %collective-permute-start.1 = (bf16[1024,128]{1,0:T(8,128)(2,1)S(1)}, bf16[1024,128]{1,0:T(8,128)(2,1)}, u32[]{:S(2)}, u32[]{:S(2)}) collective-permute-start(bf16[1024,128]{1,0:T(8,128)(2,1)S(1)} %get-tuple-element.30.raw_ref), channel_id=1, source_target_pairs={{0,16},{4,20},{8,24},{12,28},{16,0},{20,4},{24,8},{28,12},{1,17},{... | collective-permute-start | bytes 786440 | tf_op jit(solution)/shard_map/ppermute | solution.py:24
  49.8 20.8 %collective-permute-start.8 = (bf16[1024,128]{1,0:T(8,128)(2,1)S(1)}, bf16[1024,128]{1,0:T(8,128)(2,1)S(1)}, u32[]{:S(2)}, u32[]{:S(2)}) collective-permute-start(bf16[1024,128]{1,0:T(8,128)(2,1)S(1)} %shard_map.62.mine_ref.block_ref), channel_id=1, source_target_pairs={{0,8},{4,12},{8,0},{12,4},{16,24},{20,28},{24,16},{28,20},{1,9},{5... | collective-permute-start | bytes 786440 | tf_op jit(solution)/shard_map/ppermute | solution.py:24
  64.5 10.1 %collective-permute-start.4 = (bf16[1024,128]{1,0:T(8,128)(2,1)S(1)}, bf16[1024,128]{1,0:T(8,128)(2,1)S(1)}, u32[]{:S(2)}, u32[]{:S(2)}) collective-permute-start(bf16[1024,128]{1,0:T(8,128)(2,1)S(1)} %shard_map.57.mine_ref.block_ref), channel_id=1, source_target_pairs={{0,8},{4,12},{8,0},{12,4},{16,24},{20,28},{24,16},{28,20},{1,9},{5... | collective-permute-start | bytes 786440 | tf_op jit(solution)/shard_map/ppermute | solution.py:24
  70.1 10.1 %collective-permute-start.2 = (bf16[1024,128]{1,0:T(8,128)(2,1)S(1)}, bf16[1024,128]{1,0:T(8,128)(2,1)S(1)}, u32[]{:S(2)}, u32[]{:S(2)}) collective-permute-start(bf16[1024,128]{1,0:T(8,128)(2,1)S(1)} %shard_map.56.block_ref.mine_ref), channel_id=1, source_target_pairs={{0,8},{4,12},{8,0},{12,4},{16,24},{20,28},{24,16},{28,20},{1,9},{5... | collective-permute-start | bytes 786440 | tf_op jit(solution)/shard_map/ppermute | solution.py:24
  71.1 11.5 %collective-permute-start.9 = (f32[512,128]{1,0:T(8,128)S(1)}, f32[512,128]{1,0:T(8,128)S(1)}, u32[]{:S(2)}, u32[]{:S(2)}) collective-permute-start(f32[512,128]{1,0:T(8,128)S(1)} %shard_map.65), channel_id=1, source_target_pairs={{0,4},{4,0},{8,12},{12,8},{16,20},{20,16},{24,28},{28,24},{1,5},{5... | collective-permute-start | bytes 786440 | tf_op jit(solution)/shard_map/ppermute | solution.py:24
  72.0 4.5 %copy-start = (bf16[512,2048]{1,0:T(8,128)(2,1)S(1)}, bf16[512,2048]{1,0:T(8,128)(2,1)}, u32[]{:S(2)}) copy-start(bf16[512,2048]{1,0:T(8,128)(2,1)} %pad_maximum_fusion.own_ref) | copy-start | bytes 6291460
  75.1 8.9 %collective-permute-start.11 = (f32[512,128]{1,0:T(8,128)S(1)}, f32[512,128]{1,0:T(8,128)S(1)}, u32[]{:S(2)}, u32[]{:S(2)}) collective-permute-start(f32[512,128]{1,0:T(8,128)S(1)} %shard_map.68), channel_id=1, source_target_pairs={{0,4},{4,0},{8,12},{12,8},{16,20},{20,16},{24,28},{28,24},{1,5},{5... | collective-permute-start | bytes 786440 | tf_op jit(solution)/shard_map/ppermute | solution.py:24
  78.0 4.5 %copy-start.2 = (f32[256,128]{1,0:T(8,128)S(1)}, f32[256,128]{1,0:T(8,128)}, u32[]{:S(2)}) copy-start(f32[256,128]{1,0:T(8,128)} %get-tuple-element.40.cos_ref) | copy-start | bytes 393220
  80.6 2.1 %copy-start.4 = (s32[2]{0:T(128)S(1)}, s32[2]{0:T(128)}, u32[]{:S(2)}) copy-start(s32[2]{0:T(128)} %param.9) | copy-start | bytes 28
  81.0 5.6 %collective-permute-start.7 = (bf16[512,128]{1,0:T(8,128)(2,1)S(1)}, bf16[512,128]{1,0:T(8,128)(2,1)S(1)}, u32[]{:S(2)}, u32[]{:S(2)}) collective-permute-start(bf16[512,128]{1,0:T(8,128)(2,1)S(1)} %shard_map.61), channel_id=1, source_target_pairs={{0,4},{4,0},{8,12},{12,8},{16,20},{20,16},{24,28},{28,24},{1,5},{5... | collective-permute-start | bytes 393224 | tf_op jit(solution)/shard_map/ppermute | solution.py:24
  82.6 1.4 %collective-permute-start.10 = (bf16[512,128]{1,0:T(8,128)(2,1)S(1)}, bf16[512,128]{1,0:T(8,128)(2,1)S(1)}, u32[]{:S(2)}, u32[]{:S(2)}) collective-permute-start(bf16[512,128]{1,0:T(8,128)(2,1)S(1)} %shard_map.66.kv_ref), channel_id=1, source_target_pairs={{0,1},{1,0},{2,3},{3,2},{4,5},{5,4},{6,7},{7,6},{8,9},{9,8},{10,11... | collective-permute-start | bytes 393224 | tf_op jit(solution)/shard_map/ppermute | solution.py:24

commit v4 on v3

--- a/solution.py
+++ b/solution.py
@@ -66,19 +66,19 @@
     half = SEQ_LEN // 2
     scale = math.log2(math.e) / math.sqrt(HEAD_DIM)
     values = jnp.concatenate([values, jnp.ones_like(values)], axis=1)
+    every = lax.dot_general(
+        queries, keys, (((1,), (1,)), ((), ())), preferred_element_type=jnp.float32
+    )
     parts = []
     for start, stop in ((0, half), (half, SEQ_LEN)):
         rows = start + lax.broadcasted_iota(jnp.int32, (stop - start, stop), 0)
         spots = lax.broadcasted_iota(jnp.int32, (stop - start, stop), 1)
-        scores = lax.dot_general(
-            queries[start:stop], keys[:stop], (((1,), (1,)), ((), ())), preferred_element_type=jnp.float32
-        )
-        scores = jnp.where((spots <= rows) & (spots < length), scores, -1e30)
+        scores = jnp.where((spots <= rows) & (spots < length), every[start:stop, :stop], -1e30)
         top = jnp.max(scores, axis=-1, keepdims=True)
-        raised = jnp.exp2((scores - top) * scale).astype(jnp.bfloat16)
-        mixed = dot(raised, values[:stop])
-        parts.append(mixed[:, :HEAD_DIM] / mixed[:, HEAD_DIM:])
-    return jnp.concatenate(parts, axis=0)
+        parts.append(jnp.exp2((scores - top) * scale).astype(jnp.bfloat16))
+    parts[0] = jnp.concatenate([parts[0], jnp.zeros_like(parts[0])], axis=1)
+    mixed = dot(jnp.concatenate(parts, axis=0), values)
+    return mixed[:, :HEAD_DIM] / mixed[:, HEAD_DIM:]
 
 
 def choose_kernel(keep_ref, raw_ref, other_ref, out_ref, sem):

time: 88.9 us -> 88.7 us (level)
  no operation moved by 1% of the time
where the time goes in v4:
time: 88.7 us; the launch traced here: 88.4 us
  waiting for transfers between devices  56.5 us (64%)
  starting transfers between devices  13.7 us (15%)
  Pallas kernels  9.64 us (11%)
  local copies, waits for them, and re-layouts  4.76 us (5%)
  other arithmetic  2.91 us (3%)
    ppermute x12, waiting for transfers between devices, swapped(): return lax.ppermute(value, axis, pairs)  56.5 us
    ppermute x12, starting transfers between devices, swapped(): return lax.ppermute(value, axis, pairs)  13.7 us
    pallas_call x12, Pallas kernels, call(): pl.pallas_call(kernel, out_shape=outs, in_specs=[SMEM] * len(scalars) + [...  7.64 us
    pallas_call x4, Pallas kernels, choose(): pl.pallas_call(choose_kernel, out_shape=pltpu.VMEM(raw.shape, raw.dtype),...  2 us
  transfers between devices with their start and end apart: 12, of which 9 were waited for; matrix products, arithmetic and copies ran while one was open for 7% of the time, Pallas kernels for 9%

profile of v4, /device:TPU:0, one launch (start us, length us, event | category | flops | bytes accessed | tf_op | source)
XLA Modules:
  0.0 88.4 jit_solution(17256862662953092024)
XLA Ops:
  0.0 1.3 %fusion.6 = (bf16[256,1024]{1,0:T(8,128)(2,1)S(1)}, bf16[256,1024]{1,0:T(8,128)(2,1)S(1)}) fusion(bf16[512,4096]{1,0:T(8,128)(2,1)} %param.5, s32[]{:T(128)S(6)} %select_n.89, s32[]{:T(128)S(6)} %select_n.90, s32[]{:T(128)S(6)} %select_n.91), kind=kLoop, calls=%fused_computation.22 | loop fusion | bytes 2097164 | tf_op jit(solution)/shard_map/dynamic_slice | solution.py:167
  1.4 3.1 %collective-permute-start.5 = (bf16[256,2048]{1,0:T(8,128)(2,1)S(1)}, bf16[256,2048]{1,0:T(8,128)(2,1)S(1)}, u32[]{:S(2)}, u32[]{:S(2)}) collective-permute-start(bf16[256,2048]{1,0:T(8,128)(2,1)S(1)} %pad_maximum_fusion.1), channel_id=1, source_target_pairs={{0,4},{4,0},{8,12},{12,8},{16,20},{20,16},{24,28},{28,24},{1,5},{5... | collective-permute-start | bytes 3145736 | tf_op jit(solution)/shard_map/ppermute | solution.py:24
  4.5 1.2 %broadcast_select_fusion = (f32[256,128]{1,0:T(8,128)S(1)}, f32[256,128]{1,0:T(8,128)S(1)}, f32[256,128]{1,0:T(8,128)S(1)}, f32[256,128]{1,0:T(8,128)}) fusion(pred[]{:T(512)S(6)} %eq.27, f32[128]{0:T(128)S(1)} %get-tuple-element.53, f32[128]{0:T(128)S(1)} %get-tuple-element.54, f32[256]{0:T(256)S(1)} %iota_convert_fusion), kind=kLoop, calls=%fused_computation.5 | loop fusion | flops 131072 | bytes 526337 | tf_op jit(solution)/shard_map/jit(_where)/select_n | solution.py:56
  5.7 21.9 %collective-permute-done.5.first_ref = bf16[256,2048]{1,0:T(8,128)(2,1)S(1)} collective-permute-done((bf16[256,2048]{1,0:T(8,128)(2,1)S(1)}, bf16[256,2048]{1,0:T(8,128)(2,1)S(1)}, u32[]{:S(2)}, u32[]{:S(2)}) %collective-permute-start.5) | collective-permute-done | bytes 1048608 | tf_op jit(solution)/shard_map/ppermute | solution.py:24
  27.6 2.8 %collective-permute-start = (bf16[1024,128]{1,0:T(8,128)(2,1)S(1)}, bf16[1024,128]{1,0:T(8,128)(2,1)}, u32[]{:S(2)}, u32[]{:S(2)}) collective-permute-start(bf16[1024,128]{1,0:T(8,128)(2,1)S(1)} %copy-done.1), channel_id=1, source_target_pairs={{0,16},{4,20},{8,24},{12,28},{16,0},{20,4},{24,8},{28,12},{1,17},{... | collective-permute-start | bytes 786440 | tf_op jit(solution)/shard_map/ppermute | solution.py:24
  30.4 1.1 %fusion.7 = (bf16[1024,128]{1,0:T(8,128)(2,1)S(1)}, bf16[1024,128]{1,0:T(8,128)(2,1)S(1)}) fusion(bf16[1024,256]{1,0:T(8,128)(2,1)} %param.6), kind=kLoop, calls=%fused_computation.23 | loop fusion | bytes 1048576 | tf_op jit(solution)/shard_map/slice | solution.py:173
  31.6 1.7 %constant_dynamic-slice_fusion.1 = (bf16[512,1024]{1,0:T(8,128)(2,1)S(1)}, bf16[512,1024]{1,0:T(8,128)(2,1)S(1)}) fusion(bf16[512,4096]{1,0:T(8,128)(2,1)} %param.5, s32[]{:T(128)S(6)} %select_n.85, s32[]{:T(128)S(6)} %select_n.86), kind=kLoop, calls=%fused_computation.21 | loop fusion | bytes 4194312 | tf_op jit(solution)/shard_map/dynamic_slice | solution.py:169
  33.3 9.8 %collective-permute-done.other_ref = bf16[1024,128]{1,0:T(8,128)(2,1)} collective-permute-done((bf16[1024,128]{1,0:T(8,128)(2,1)S(1)}, bf16[1024,128]{1,0:T(8,128)(2,1)}, u32[]{:S(2)}, u32[]{:S(2)}) %collective-permute-start) | collective-permute-done | bytes 262176 | tf_op jit(solution)/shard_map/ppermute | solution.py:24
  43.1 1.5 %pad_maximum_fusion.own_ref = bf16[512,2048]{1,0:T(8,128)(2,1)} fusion(bf16[512,1024]{1,0:T(8,128)(2,1)S(1)} %get-tuple-element.46, bf16[512,1024]{1,0:T(8,128)(2,1)S(1)} %get-tuple-element.45), kind=kLoop, calls=%fused_computation | loop fusion | flops 4194304 | bytes 4194304 | tf_op jit(solution)/shard_map/concatenate | solution.py:170
  44.7 2.9 %collective-permute-start.1 = (bf16[1024,128]{1,0:T(8,128)(2,1)S(1)}, bf16[1024,128]{1,0:T(8,128)(2,1)}, u32[]{:S(2)}, u32[]{:S(2)}) collective-permute-start(bf16[1024,128]{1,0:T(8,128)(2,1)S(1)} %get-tuple-element.30.raw_ref), channel_id=1, source_target_pairs={{0,16},{4,20},{8,24},{12,28},{16,0},{20,4},{24,8},{28,12},{1,17},{... | collective-permute-start | bytes 786440 | tf_op jit(solution)/shard_map/ppermute | solution.py:24
  47.6 0.6 dynamic_slice.17
  48.9 1.0 %shard_map.62.mine_ref.block_ref = bf16[1024,128]{1,0:T(8,128)(2,1)S(1)} custom-call(s32[1]{0:T(128)} %bitcast.2.keep_ref, bf16[1024,128]{1,0:T(8,128)(2,1)S(1)} %shard_map.55.raw_ref, bf16[1024,128]{1,0:T(8,128)(2,1)} %collective-permute-done.other_ref), custom_call_target="tpu_custom_call" | custom-call | bytes 524288 | tf_op jit(solution)/shard_map/pallas_call | solution.py:95
  49.8 1.2 %collective-permute-start.8 = (bf16[1024,128]{1,0:T(8,128)(2,1)S(1)}, bf16[1024,128]{1,0:T(8,128)(2,1)S(1)}, u32[]{:S(2)}, u32[]{:S(2)}) collective-permute-start(bf16[1024,128]{1,0:T(8,128)(2,1)S(1)} %shard_map.62.mine_ref.block_ref), channel_id=1, source_target_pairs={{0,8},{4,12},{8,0},{12,4},{16,24},{20,28},{24,16},{28,20},{1,9},{5... | collective-permute-start | bytes 786440 | tf_op jit(solution)/shard_map/ppermute | solution.py:24
  51.1 13.4 %collective-permute-done.3.other_ref = bf16[1024,128]{1,0:T(8,128)(2,1)S(1)} collective-permute-done((bf16[1024,128]{1,0:T(8,128)(2,1)S(1)}, bf16[1024,128]{1,0:T(8,128)(2,1)S(1)}, u32[]{:S(2)}, u32[]{:S(2)}) %collective-permute-start.3) | collective-permute-done | bytes 262176 | tf_op jit(solution)/shard_map/ppermute | solution.py:24
  64.6 4.6 %collective-permute-done.1.other_ref = bf16[1024,128]{1,0:T(8,128)(2,1)} collective-permute-done((bf16[1024,128]{1,0:T(8,128)(2,1)S(1)}, bf16[1024,128]{1,0:T(8,128)(2,1)}, u32[]{:S(2)}, u32[]{:S(2)}) %collective-permute-start.1) | collective-permute-done | bytes 262176 | tf_op jit(solution)/shard_map/ppermute | solution.py:24
  69.1 1.0 %shard_map.56.block_ref.mine_ref = bf16[1024,128]{1,0:T(8,128)(2,1)S(1)} custom-call(s32[1]{0:T(128)} %bitcast.2.keep_ref, bf16[1024,128]{1,0:T(8,128)(2,1)S(1)} %get-tuple-element.30.raw_ref, bf16[1024,128]{1,0:T(8,128)(2,1)} %collective-permute-done.1.other_ref), custom_call_target="tpu_custom_call" | custom-call | bytes 524288 | tf_op jit(solution)/shard_map/pallas_call | solution.py:95
  70.2 0.4 shard_map.64.refs_0_
  70.6 0.4 shard_map.65
  71.1 0.5 collective-permute-start.9
  72.0 2.6 %collective-permute-done.4.far_ref.block_ref = bf16[1024,128]{1,0:T(8,128)(2,1)S(1)} collective-permute-done((bf16[1024,128]{1,0:T(8,128)(2,1)S(1)}, bf16[1024,128]{1,0:T(8,128)(2,1)S(1)}, u32[]{:S(2)}, u32[]{:S(2)}) %collective-permute-start.4) | collective-permute-done | bytes 262176 | tf_op jit(solution)/shard_map/ppermute | solution.py:24
  75.1 1.5 %collective-permute-start.11 = (f32[512,128]{1,0:T(8,128)S(1)}, f32[512,128]{1,0:T(8,128)S(1)}, u32[]{:S(2)}, u32[]{:S(2)}) collective-permute-start(f32[512,128]{1,0:T(8,128)S(1)} %shard_map.68), channel_id=1, source_target_pairs={{0,4},{4,0},{8,12},{12,8},{16,20},{20,16},{24,28},{28,24},{1,5},{5... | collective-permute-start | bytes 786440 | tf_op jit(solution)/shard_map/ppermute | solution.py:24
  76.5 0.7 shard_map.63.own_ref
  77.3 0.7 shard_map.58.own_ref
  78.0 2.2 %collective-permute-done.2.far_ref.block_ref = bf16[1024,128]{1,0:T(8,128)(2,1)S(1)} collective-permute-done((bf16[1024,128]{1,0:T(8,128)(2,1)S(1)}, bf16[1024,128]{1,0:T(8,128)(2,1)S(1)}, u32[]{:S(2)}, u32[]{:S(2)}) %collective-permute-start.2) | collective-permute-done | bytes 262176 | tf_op jit(solution)/shard_map/ppermute | solution.py:24
  80.2 0.4 shard_map.59.refs_0_
  80.6 0.4 shard_map.61
  81.0 1.5 %collective-permute-start.7 = (bf16[512,128]{1,0:T(8,128)(2,1)S(1)}, bf16[512,128]{1,0:T(8,128)(2,1)S(1)}, u32[]{:S(2)}, u32[]{:S(2)}) collective-permute-start(bf16[512,128]{1,0:T(8,128)(2,1)S(1)} %shard_map.61), channel_id=1, source_target_pairs={{0,4},{4,0},{8,12},{12,8},{16,20},{20,16},{24,28},{28,24},{1,5},{5... | collective-permute-start | bytes 393224 | tf_op jit(solution)/shard_map/ppermute | solution.py:24
  82.8 0.7 shard_map.60.own_ref
  83.5 0.5 collective-permute-done.11.sent_ref
  84.1 1.1 %shard_map.69.refs_0_ = bf16[512,128]{1,0:T(8,128)(2,1)S(1)} custom-call(s32[3]{0:T(128)S(1)} %pad_add_fusion.facts_ref, f32[512,128]{1,0:T(8,128)S(1)} %shard_map.58.own_ref, f32[512,128]{1,0:T(8,128)S(1)} %collective-permute-done.11.sent_ref, f32[256,128]{1,0:T(8,128)S(1)} %get-tuple-element.36.cos_ref, f32[256,128]{1,0:T(8,128)S(1)} %get-tuple-element.37.sin_ref, ...), custom_call_target="tpu_custom_call" | custom-call | flops 67108864 | bytes 262144 | tf_op jit(solution)/shard_map/pallas_call | solution.py:36
  85.2 1.5 %collective-permute-done.7.sent_ref = bf16[512,128]{1,0:T(8,128)(2,1)S(1)} collective-permute-done((bf16[512,128]{1,0:T(8,128)(2,1)S(1)}, bf16[512,128]{1,0:T(8,128)(2,1)S(1)}, u32[]{:S(2)}, u32[]{:S(2)}) %collective-permute-start.7) | collective-permute-done | bytes 131104 | tf_op jit(solution)/shard_map/ppermute | solution.py:24
  86.7 1.7 %shard_map.70 = bf16[512,256]{1,0:T(8,128)(2,1)} custom-call(s32[3]{0:T(128)S(1)} %pad_add_fusion.facts_ref, f32[512,128]{1,0:T(8,128)S(1)} %shard_map.60.own_ref, bf16[512,128]{1,0:T(8,128)(2,1)S(1)} %collective-permute-done.7.sent_ref, f32[256,128]{1,0:T(8,128)S(1)} %get-tuple-element.36.cos_ref, f32[256,128]{1,0:T(8,128)S(1)} %get-tuple-element.37.sin_ref, ...), custom_call_target="tpu_custom_call" | custom-call | flops 67108864 | bytes 262144 | tf_op jit(solution)/shard_map/pallas_call | solution.py:36
  (28 shorter events, 1.5 us)
Async XLA Ops:
  0.0 27.6 %copy-start.1 = (bf16[1024,128]{1,0:T(8,128)(2,1)S(1)}, bf16[1024,128]{1,0:T(8,128)(2,1)}, u32[]{:S(2)}) copy-start(bf16[1024,128]{1,0:T(8,128)(2,1)} %other_ref.1) | copy-start | bytes 786436
  1.4 26.2 %collective-permute-start.5 = (bf16[256,2048]{1,0:T(8,128)(2,1)S(1)}, bf16[256,2048]{1,0:T(8,128)(2,1)S(1)}, u32[]{:S(2)}, u32[]{:S(2)}) collective-permute-start(bf16[256,2048]{1,0:T(8,128)(2,1)S(1)} %pad_maximum_fusion.1), channel_id=1, source_target_pairs={{0,4},{4,0},{8,12},{12,8},{16,20},{20,16},{24,28},{28,24},{1,5},{5... | collective-permute-start | bytes 3145736 | tf_op jit(solution)/shard_map/ppermute | solution.py:24
  27.6 42.5 %collective-permute-start.6 = (bf16[256,2048]{1,0:T(8,128)(2,1)S(1)}, bf16[256,2048]{1,0:T(8,128)(2,1)S(1)}, u32[]{:S(2)}, u32[]{:S(2)}) collective-permute-start(bf16[256,2048]{1,0:T(8,128)(2,1)S(1)} %collective-permute-done.5.first_ref), channel_id=1, source_target_pairs={{0,1},{1,0},{2,3},{3,2},{4,5},{5,4},{6,7},{7,6},{8,9},{9,8},{10,11... | collective-permute-start | bytes 3145736 | tf_op jit(solution)/shard_map/ppermute | solution.py:24
  27.6 15.5 %collective-permute-start = (bf16[1024,128]{1,0:T(8,128)(2,1)S(1)}, bf16[1024,128]{1,0:T(8,128)(2,1)}, u32[]{:S(2)}, u32[]{:S(2)}) collective-permute-start(bf16[1024,128]{1,0:T(8,128)(2,1)S(1)} %copy-done.1), channel_id=1, source_target_pairs={{0,16},{4,20},{8,24},{12,28},{16,0},{20,4},{24,8},{28,12},{1,17},{... | collective-permute-start | bytes 786440 | tf_op jit(solution)/shard_map/ppermute | solution.py:24
  43.1 21.3 %collective-permute-start.3 = (bf16[1024,128]{1,0:T(8,128)(2,1)S(1)}, bf16[1024,128]{1,0:T(8,128)(2,1)S(1)}, u32[]{:S(2)}, u32[]{:S(2)}) collective-permute-start(bf16[1024,128]{1,0:T(8,128)(2,1)S(1)} %get-tuple-element.31.raw_ref), channel_id=1, source_target_pairs={{0,16},{4,20},{8,24},{12,28},{16,0},{20,4},{24,8},{28,12},{1,17},{... | collective-permute-start | bytes 786440 | tf_op jit(solution)/shard_map/ppermute | solution.py:24
  43.1 4.4 %copy-start.3 = (s32[4]{0:T(128)S(1)}, s32[4]{0:T(128)}, u32[]{:S(2)}) copy-start(s32[4]{0:T(128)} %param.8) | copy-start | bytes 52
  44.7 24.5 %collective-permute-start.1 = (bf16[1024,128]{1,0:T(8,128)(2,1)S(1)}, bf16[1024,128]{1,0:T(8,128)(2,1)}, u32[]{:S(2)}, u32[]{:S(2)}) collective-permute-start(bf16[1024,128]{1,0:T(8,128)(2,1)S(1)} %get-tuple-element.30.raw_ref), channel_id=1, source_target_pairs={{0,16},{4,20},{8,24},{12,28},{16,0},{20,4},{24,8},{28,12},{1,17},{... | collective-permute-start | bytes 786440 | tf_op jit(solution)/shard_map/ppermute | solution.py:24
  49.8 20.8 %collective-permute-start.8 = (bf16[1024,128]{1,0:T(8,128)(2,1)S(1)}, bf16[1024,128]{1,0:T(8,128)(2,1)S(1)}, u32[]{:S(2)}, u32[]{:S(2)}) collective-permute-start(bf16[1024,128]{1,0:T(8,128)(2,1)S(1)} %shard_map.62.mine_ref.block_ref), channel_id=1, source_target_pairs={{0,8},{4,12},{8,0},{12,4},{16,24},{20,28},{24,16},{28,20},{1,9},{5... | collective-permute-start | bytes 786440 | tf_op jit(solution)/shard_map/ppermute | solution.py:24
  64.5 10.1 %collective-permute-start.4 = (bf16[1024,128]{1,0:T(8,128)(2,1)S(1)}, bf16[1024,128]{1,0:T(8,128)(2,1)S(1)}, u32[]{:S(2)}, u32[]{:S(2)}) collective-permute-start(bf16[1024,128]{1,0:T(8,128)(2,1)S(1)} %shard_map.57.mine_ref.block_ref), channel_id=1, source_target_pairs={{0,8},{4,12},{8,0},{12,4},{16,24},{20,28},{24,16},{28,20},{1,9},{5... | collective-permute-start | bytes 786440 | tf_op jit(solution)/shard_map/ppermute | solution.py:24
  70.1 10.1 %collective-permute-start.2 = (bf16[1024,128]{1,0:T(8,128)(2,1)S(1)}, bf16[1024,128]{1,0:T(8,128)(2,1)S(1)}, u32[]{:S(2)}, u32[]{:S(2)}) collective-permute-start(bf16[1024,128]{1,0:T(8,128)(2,1)S(1)} %shard_map.56.block_ref.mine_ref), channel_id=1, source_target_pairs={{0,8},{4,12},{8,0},{12,4},{16,24},{20,28},{24,16},{28,20},{1,9},{5... | collective-permute-start | bytes 786440 | tf_op jit(solution)/shard_map/ppermute | solution.py:24
  71.1 11.5 %collective-permute-start.9 = (f32[512,128]{1,0:T(8,128)S(1)}, f32[512,128]{1,0:T(8,128)S(1)}, u32[]{:S(2)}, u32[]{:S(2)}) collective-permute-start(f32[512,128]{1,0:T(8,128)S(1)} %shard_map.65), channel_id=1, source_target_pairs={{0,4},{4,0},{8,12},{12,8},{16,20},{20,16},{24,28},{28,24},{1,5},{5... | collective-permute-start | bytes 786440 | tf_op jit(solution)/shard_map/ppermute | solution.py:24
  72.0 4.5 %copy-start = (bf16[512,2048]{1,0:T(8,128)(2,1)S(1)}, bf16[512,2048]{1,0:T(8,128)(2,1)}, u32[]{:S(2)}) copy-start(bf16[512,2048]{1,0:T(8,128)(2,1)} %pad_maximum_fusion.own_ref) | copy-start | bytes 6291460
  75.1 8.9 %collective-permute-start.11 = (f32[512,128]{1,0:T(8,128)S(1)}, f32[512,128]{1,0:T(8,128)S(1)}, u32[]{:S(2)}, u32[]{:S(2)}) collective-permute-start(f32[512,128]{1,0:T(8,128)S(1)} %shard_map.68), channel_id=1, source_target_pairs={{0,4},{4,0},{8,12},{12,8},{16,20},{20,16},{24,28},{28,24},{1,5},{5... | collective-permute-start | bytes 786440 | tf_op jit(solution)/shard_map/ppermute | solution.py:24
  78.0 4.5 %copy-start.2 = (f32[256,128]{1,0:T(8,128)S(1)}, f32[256,128]{1,0:T(8,128)}, u32[]{:S(2)}) copy-start(f32[256,128]{1,0:T(8,128)} %get-tuple-element.40.cos_ref) | copy-start | bytes 393220
  80.6 2.1 %copy-start.4 = (s32[2]{0:T(128)S(1)}, s32[2]{0:T(128)}, u32[]{:S(2)}) copy-start(s32[2]{0:T(128)} %param.9) | copy-start | bytes 28
  81.0 5.6 %collective-permute-start.7 = (bf16[512,128]{1,0:T(8,128)(2,1)S(1)}, bf16[512,128]{1,0:T(8,128)(2,1)S(1)}, u32[]{:S(2)}, u32[]{:S(2)}) collective-permute-start(bf16[512,128]{1,0:T(8,128)(2,1)S(1)} %shard_map.61), channel_id=1, source_target_pairs={{0,4},{4,0},{8,12},{12,8},{16,20},{20,16},{24,28},{28,24},{1,5},{5... | collective-permute-start | bytes 393224 | tf_op jit(solution)/shard_map/ppermute | solution.py:24
  82.6 1.4 %collective-permute-start.10 = (bf16[512,128]{1,0:T(8,128)(2,1)S(1)}, bf16[512,128]{1,0:T(8,128)(2,1)S(1)}, u32[]{:S(2)}, u32[]{:S(2)}) collective-permute-start(bf16[512,128]{1,0:T(8,128)(2,1)S(1)} %shard_map.66.kv_ref), channel_id=1, source_target_pairs={{0,1},{1,0},{2,3},{3,2},{4,5},{5,4},{6,7},{7,6},{8,9},{9,8},{10,11... | collective-permute-start | bytes 393224 | tf_op jit(solution)/shard_map/ppermute | solution.py:24
